TPU v7x, 128 devices: a whole 4x4x4 slice. The times are simulated.
128 devices in a mesh: frames: 2 (over core), prow: 8 (over z_lo, x), pcol: 8 (over y, z_hi).
Axes of the slice: x: 4, y: 4, z: 4 (z_hi: 2, z_lo: 2; z = z_hi * 2 + z_lo), core: 2. Of those that a mesh axis runs over, the one named last changes fastest.
Arguments:
- poses: bfloat16 [262144, 256], P(('frames', 'prow', 'pcol')), may hold values from -6 to 6
- codebook: bfloat16 [32, 256], replicated, may hold values from -4 to 4
- offsets: bfloat16 [32, 256], replicated, may hold values from -4 to 4
- confidence: float32 [262144], P(('frames', 'prow', 'pcol')), may hold values from 0.2 to 1
- code_ids: int32 [262144], P(('frames', 'prow', 'pcol')), may hold values from 0 to 31
- creature_ids: int32 [262144], P(('frames', 'prow', 'pcol')), may hold values from 0 to 31
- hess_raw: float32 [8, 8, 128, 8, 8, 128], P(None, 'prow', None, None, 'pcol'), may hold values from -1 to 1, as said below
- pattern: int32 [64, 64], replicated, may hold values from 0 to 1, as said below
- membership: int32 [2, 2], replicated, may hold values from 0 to 63, as said below
Outputs:
- factor_state: float32 [8, 8, 128, 8, 8, 128], P(None, 'prow', None, None, 'pcol')
- reduced_grad: float32 [8, 8, 128], P(None, 'prow')
Inputs may be any that keep to these rules, and one draw needn't show every extreme that they name: As an 8192 x 8192 matrix hess_raw is symmetric. pattern is symmetric with ones on its diagonal. Within each row of membership all pattern entries are one, and for every block row i outside a supernode, pattern[i, p] is the same for all block columns p of that supernode. The 4 entries of membership are distinct block indices.
All inputs are finite; a program needn't handle non-finite values.
Results may differ from a plain program's by a relative error of at most 0.0003.
Values sent between devices are 32-bit elements; how exact they have to be, the bound alone decides.
A program may use at most 64 MiB of HBM per device.

v0:
```python
import math

import jax
import jax.numpy as jnp
from jax import lax
from jax.sharding import PartitionSpec as P

NPAN = 8192


precise = lax.Precision.HIGHEST


def from_root(value, axis, source):
    kept = jnp.where(lax.axis_index(axis) == source, value, 0).astype(value.dtype)
    return lax.psum(kept, axis)


def solve_rows(factor_blk, column):
    blocksize = factor_blk.shape[0]
    block_count = column.shape[0]
    right_side = jnp.transpose(column, (2, 0, 1)).reshape(blocksize, block_count * blocksize)
    solution = jax.scipy.linalg.solve_triangular(factor_blk, right_side, lower=True)
    return jnp.transpose(solution.reshape(blocksize, block_count, blocksize), (1, 2, 0))


def shards(
    poses, codebook, offsets, confidence, code_ids, creature_ids, hess_raw, pattern, membership
):
    grid_rows = lax.axis_size("prow")
    grid_cols = lax.axis_size("pcol")
    my_row = lax.axis_index("prow")
    my_col = lax.axis_index("pcol")
    code_count = codebook.shape[0]
    kind_count = offsets.shape[0]
    local_rows = hess_raw.shape[0]
    local_cols = hess_raw.shape[3]
    blocksize = hess_raw.shape[2]
    code_table = (code_ids[None, :] == jnp.arange(code_count, dtype=jnp.int32)[:, None]).astype(
        jnp.float32
    )
    kind_table = (creature_ids[None, :] == jnp.arange(kind_count, dtype=jnp.int32)[:, None]).astype(
        jnp.float32
    )
    predicted = jnp.einsum("cf,cw->fw", code_table, codebook.astype(jnp.float32), precision=precise)
    predicted = predicted + jnp.einsum(
        "cf,cw->fw", kind_table, offsets.astype(jnp.float32), precision=precise
    )
    residual = confidence[:, None] * (poses.astype(jnp.float32) - predicted)
    frame_total = poses.shape[0] * lax.axis_size("frames") * grid_rows * grid_cols
    partial_grad = jnp.einsum("cf,fw->cw", code_table, residual, precision=precise) / math.sqrt(
        frame_total / code_count
    )
    partial_grad = partial_grad.reshape(local_rows, grid_rows, blocksize)
    summed = lax.psum(partial_grad, ("frames", "prow", "pcol"))
    grad_local = lax.dynamic_index_in_dim(summed, my_row, 1, False)
    shift = 2.5 * math.sqrt(NPAN)
    local_pattern = pattern.reshape(local_rows, grid_rows, local_cols, grid_cols)
    local_pattern = lax.dynamic_index_in_dim(local_pattern, my_row, 1, False)
    local_pattern = lax.dynamic_index_in_dim(local_pattern, my_col, 2, False)
    mask_four = local_pattern.astype(jnp.float32)[:, None, :, None]
    row_ids = jnp.arange(local_rows, dtype=jnp.int32) * grid_rows + my_row
    col_ids = jnp.arange(local_cols, dtype=jnp.int32) * grid_cols + my_col
    same_block = (row_ids[:, None] == col_ids[None, :]).astype(jnp.float32)
    identity = jnp.eye(blocksize, dtype=jnp.float32)
    matrix = (
        hess_raw[:, 0, :, :, 0, :] * mask_four
        + shift * same_block[:, None, :, None] * identity[None, :, None, :]
    )
    order = membership.reshape(-1)

    def eliminate(position, state_pair):
        matrix, grad_local = state_pair
        pivot = order[position]
        pivot_row = pivot % grid_rows
        pivot_col = pivot % grid_cols
        slot_row = pivot // grid_rows
        slot_col = pivot // grid_cols
        on_row = my_row == pivot_row
        on_col = my_col == pivot_col
        diag_here = lax.dynamic_index_in_dim(
            lax.dynamic_index_in_dim(matrix, slot_row, 0, False), slot_col, 1, False
        )
        grad_here = lax.dynamic_index_in_dim(grad_local, slot_row, 0, False)
        diag_blk, grad_blk = (
            from_root(diag_here, ("prow", "pcol"), pivot_row * grid_cols + pivot_col),
            from_root(grad_here, ("prow", "pcol"), pivot_row * grid_cols + pivot_col),
        )
        factor_blk = jnp.linalg.cholesky(diag_blk)
        solved = jax.scipy.linalg.solve_triangular(factor_blk, grad_blk, lower=True)
        column = lax.dynamic_index_in_dim(matrix, slot_col, 2, False)
        column = column * (row_ids != pivot).astype(jnp.float32)[:, None, None]
        panel_rows = from_root(solve_rows(factor_blk, column), "pcol", pivot_col)
        mirrored = from_root(panel_rows, "prow", my_col)
        matrix = matrix - mask_four * jnp.einsum(
            "ixk,jyk->ixjy", panel_rows, mirrored, precision=precise
        )
        grad_local = grad_local - jnp.einsum("ixk,k->ix", panel_rows, solved, precision=precise)
        grad_local = jnp.where(
            on_row, lax.dynamic_update_index_in_dim(grad_local, solved, slot_row, 0), grad_local
        )
        row_block = lax.dynamic_index_in_dim(matrix, slot_row, 0, False)
        matrix = lax.dynamic_update_index_in_dim(
            matrix, jnp.where(on_row, jnp.zeros_like(row_block), row_block), slot_row, 0
        )
        col_block = lax.dynamic_index_in_dim(matrix, slot_col, 2, False)
        filled = jnp.where(
            on_row, lax.dynamic_update_index_in_dim(panel_rows, factor_blk, slot_row, 0), panel_rows
        )
        matrix = lax.dynamic_update_index_in_dim(
            matrix, jnp.where(on_col, filled, col_block), slot_col, 2
        )
        return (matrix, grad_local)

    matrix, grad_local = lax.fori_loop(0, order.shape[0], eliminate, (matrix, grad_local))
    return (matrix[:, None, :, :, None, :], grad_local[:, None, :])


def solution(mesh):
    return jax.shard_map(
        shards,
        mesh=mesh,
        in_specs=(
            P(("frames", "prow", "pcol"), None),
            P(),
            P(),
            P(("frames", "prow", "pcol")),
            P(("frames", "prow", "pcol")),
            P(("frames", "prow", "pcol")),
            P(None, "prow", None, None, "pcol", None),
            P(),
            P(),
        ),
        out_specs=(P(None, "prow", None, None, "pcol", None), P(None, "prow", None)),
        check_vma=False,
    )
```

profile of v0, /device:TPU:105, one launch (start us, length us, event | category | flops | bytes accessed | tf_op | source)
XLA Modules:
  0.0 1791.8 jit_solution(806905055227306704)
XLA Ops:
  13.3 64.5 %psum.67 = f32[8,8,128]{2,1,0:T(8,128)S(1)} all-reduce(f32[8,8,128]{2,1,0:T(8,128)S(1)} %reshape.143), channel_id=1, replica_groups=mesh['frames'=2,'prow'=8,'pcol'=8] {'frames','prow','pcol'}, use_global_device_ids=true, to_apply=%region_0.0 | all-reduce | flops 8192 | bytes 65536 | tf_op jit(solution)/shard_map/psum | solution.py:55
  77.8 10.9 copy.33
  93.4 1686.3 %while.20 = (s32[]{:T(128)}, f32[8,128,8,128]{1,3,2,0:T(8,128)}, f32[8,128]{1,0:T(8,128)S(1)}, f32[8,1,8,1]{2,0,3,1:T(8,128)S(1)}, s32[4]{0:T(128)S(1)}, /*index...) while((s32[]{:T(128)}, f32[8,128,8,128]{1,3,2,0:T(8,128)}, ...), condition=%wide.region_8.9_spmd.clone.clone, body=%wide.region_1.8_spmd.clone.clone.sunk | while | flops 1816970880 | bytes 44392472 | solution.py:115
  99.7 116.7 %all-reduce.4.cloned.1.call-done = f32[128,128]{0,1:T(8,128)} async-done(((f32[128,128]{0,1:T(8,128)}), f32[128,128]{0,1:T(8,128)}) %all-reduce.4.cloned.1.call-update) | async-done | bytes 65552 | tf_op jit(solution)/shard_map/while/body/eval_jaxpr/psum | solution.py:16
  218.2 11.7 cholesky.80
  231.4 9.8 custom-call.29
  242.7 5.3 copy.44
  248.1 124.9 %psum.83 = f32[128]{0:T(128)S(1)} all-reduce(f32[128]{0:T(128)S(1)} %fusion.50), channel_id=1, replica_groups=mesh['frames'=2,'prow'=8,'pcol'=8] {'prow','pcol'}, use_global_device_ids=true, to_apply=%region_7.7 | all-reduce | flops 128 | bytes 1024 | tf_op jit(solution)/shard_map/while/body/eval_jaxpr/psum | solution.py:16
  375.7 116.4 %all-reduce.8.cloned.1.call-done = f32[8,128,128]{2,1,0:T(8,128)} async-done(((f32[8,128,128]{2,1,0:T(8,128)}), f32[8,128,128]{2,1,0:T(8,128)}) %all-reduce.8.cloned.1.call-update) | async-done | bytes 524304 | tf_op jit(solution)/shard_map/while/body/eval_jaxpr/psum | solution.py:16
  492.1 8.2 multiply_subtract_fusion.2
  504.8 5.3 copy.47
  516.4 123.0 %all-reduce.4.cloned.1.call-done = f32[128,128]{0,1:T(8,128)} async-done(((f32[128,128]{0,1:T(8,128)}), f32[128,128]{0,1:T(8,128)}) %all-reduce.4.cloned.1.call-update) | async-done | bytes 65552 | tf_op jit(solution)/shard_map/while/body/eval_jaxpr/psum | solution.py:16
  641.2 11.7 cholesky.80
  654.4 9.8 custom-call.29
  671.1 124.9 %psum.83 = f32[128]{0:T(128)S(1)} all-reduce(f32[128]{0:T(128)S(1)} %fusion.50), channel_id=1, replica_groups=mesh['frames'=2,'prow'=8,'pcol'=8] {'prow','pcol'}, use_global_device_ids=true, to_apply=%region_7.7 | all-reduce | flops 128 | bytes 1024 | tf_op jit(solution)/shard_map/while/body/eval_jaxpr/psum | solution.py:16
  798.7 116.4 %all-reduce.8.cloned.1.call-done = f32[8,128,128]{2,1,0:T(8,128)} async-done(((f32[8,128,128]{2,1,0:T(8,128)}), f32[8,128,128]{2,1,0:T(8,128)}) %all-reduce.8.cloned.1.call-update) | async-done | bytes 524304 | tf_op jit(solution)/shard_map/while/body/eval_jaxpr/psum | solution.py:16
  915.2 8.2 multiply_subtract_fusion.2
  927.9 5.3 copy.47
  939.5 123.3 %all-reduce.4.cloned.1.call-done = f32[128,128]{0,1:T(8,128)} async-done(((f32[128,128]{0,1:T(8,128)}), f32[128,128]{0,1:T(8,128)}) %all-reduce.4.cloned.1.call-update) | async-done | bytes 65552 | tf_op jit(solution)/shard_map/while/body/eval_jaxpr/psum | solution.py:16
  1064.6 11.7 cholesky.80
  1077.8 9.8 custom-call.29
  1094.5 124.9 %psum.83 = f32[128]{0:T(128)S(1)} all-reduce(f32[128]{0:T(128)S(1)} %fusion.50), channel_id=1, replica_groups=mesh['frames'=2,'prow'=8,'pcol'=8] {'prow','pcol'}, use_global_device_ids=true, to_apply=%region_7.7 | all-reduce | flops 128 | bytes 1024 | tf_op jit(solution)/shard_map/while/body/eval_jaxpr/psum | solution.py:16
  1222.1 116.4 %all-reduce.8.cloned.1.call-done = f32[8,128,128]{2,1,0:T(8,128)} async-done(((f32[8,128,128]{2,1,0:T(8,128)}), f32[8,128,128]{2,1,0:T(8,128)}) %all-reduce.8.cloned.1.call-update) | async-done | bytes 524304 | tf_op jit(solution)/shard_map/while/body/eval_jaxpr/psum | solution.py:16
  1338.5 8.2 multiply_subtract_fusion.2
  1351.2 5.3 copy.47
  1362.8 123.0 %all-reduce.4.cloned.1.call-done = f32[128,128]{0,1:T(8,128)} async-done(((f32[128,128]{0,1:T(8,128)}), f32[128,128]{0,1:T(8,128)}) %all-reduce.4.cloned.1.call-update) | async-done | bytes 65552 | tf_op jit(solution)/shard_map/while/body/eval_jaxpr/psum | solution.py:16
  1487.6 11.7 cholesky.80
  1500.8 9.8 custom-call.29
  1517.5 124.9 %psum.83 = f32[128]{0:T(128)S(1)} all-reduce(f32[128]{0:T(128)S(1)} %fusion.50), channel_id=1, replica_groups=mesh['frames'=2,'prow'=8,'pcol'=8] {'prow','pcol'}, use_global_device_ids=true, to_apply=%region_7.7 | all-reduce | flops 128 | bytes 1024 | tf_op jit(solution)/shard_map/while/body/eval_jaxpr/psum | solution.py:16
  1645.1 116.5 %all-reduce.8.cloned.1.call-done = f32[8,128,128]{2,1,0:T(8,128)} async-done(((f32[8,128,128]{2,1,0:T(8,128)}), f32[8,128,128]{2,1,0:T(8,128)}) %all-reduce.8.cloned.1.call-update) | async-done | bytes 524304 | tf_op jit(solution)/shard_map/while/body/eval_jaxpr/psum | solution.py:16
  1761.6 8.2 multiply_subtract_fusion.2
  1774.3 5.3 copy.47
  (147 shorter events, 95.8 us)
Async XLA Ops:
  7.2 2.1 copy-start
  7.2 5.2 copy-start.3
  93.4 123.0 %all-reduce.4.cloned.1.call-start = ((), (), s32[]{:S(2)}) async-start(), calls=%async_computation | async-start | bytes 131072 | tf_op jit(solution)/shard_map/while/body/eval_jaxpr/psum | solution.py:16
  97.7 275.3 %all-reduce.6.cloned.1.call-start = ((), (), s32[]{:S(2)}) async-start(), calls=%async_computation.1 | async-start | bytes 1048576 | tf_op jit(solution)/shard_map/while/body/eval_jaxpr/psum | solution.py:16
  242.7 249.4 %all-reduce.8.cloned.1.call-start = ((), (), s32[]{:S(2)}) async-start(), calls=%async_computation.2 | async-start | bytes 1048576 | tf_op jit(solution)/shard_map/while/body/eval_jaxpr/psum | solution.py:16
  492.1 11.1 copy-start.1
  510.1 129.3 %all-reduce.4.cloned.1.call-start = ((), (), s32[]{:S(2)}) async-start(), calls=%async_computation | async-start | bytes 131072 | tf_op jit(solution)/shard_map/while/body/eval_jaxpr/psum | solution.py:16
  514.5 281.5 %all-reduce.6.cloned.1.call-start = ((), (), s32[]{:S(2)}) async-start(), calls=%async_computation.1 | async-start | bytes 1048576 | tf_op jit(solution)/shard_map/while/body/eval_jaxpr/psum | solution.py:16
  665.7 249.5 %all-reduce.8.cloned.1.call-start = ((), (), s32[]{:S(2)}) async-start(), calls=%async_computation.2 | async-start | bytes 1048576 | tf_op jit(solution)/shard_map/while/body/eval_jaxpr/psum | solution.py:16
  915.2 11.1 copy-start.1
  933.2 129.6 %all-reduce.4.cloned.1.call-start = ((), (), s32[]{:S(2)}) async-start(), calls=%async_computation | async-start | bytes 131072 | tf_op jit(solution)/shard_map/while/body/eval_jaxpr/psum | solution.py:16
  937.6 281.8 %all-reduce.6.cloned.1.call-start = ((), (), s32[]{:S(2)}) async-start(), calls=%async_computation.1 | async-start | bytes 1048576 | tf_op jit(solution)/shard_map/while/body/eval_jaxpr/psum | solution.py:16
  1089.0 249.4 %all-reduce.8.cloned.1.call-start = ((), (), s32[]{:S(2)}) async-start(), calls=%async_computation.2 | async-start | bytes 1048576 | tf_op jit(solution)/shard_map/while/body/eval_jaxpr/psum | solution.py:16
  1338.5 11.1 copy-start.1
  1356.5 129.3 %all-reduce.4.cloned.1.call-start = ((), (), s32[]{:S(2)}) async-start(), calls=%async_computation | async-start | bytes 131072 | tf_op jit(solution)/shard_map/while/body/eval_jaxpr/psum | solution.py:16
  1360.9 281.5 %all-reduce.6.cloned.1.call-start = ((), (), s32[]{:S(2)}) async-start(), calls=%async_computation.1 | async-start | bytes 1048576 | tf_op jit(solution)/shard_map/while/body/eval_jaxpr/psum | solution.py:16
  1512.1 249.5 %all-reduce.8.cloned.1.call-start = ((), (), s32[]{:S(2)}) async-start(), calls=%async_computation.2 | async-start | bytes 1048576 | tf_op jit(solution)/shard_map/while/body/eval_jaxpr/psum | solution.py:16
  1761.6 11.1 copy-start.1
  1779.7 5.3 copy-start.2
Sparse Core Ops, SparseCore 0:
  99.5 116.8 all-reduce.3
  242.8 78.9 all-reduce.5
  374.0 118.0 all-reduce.7
  515.9 123.4 all-reduce.3
  665.8 78.9 all-reduce.5
  797.0 118.0 all-reduce.7
  939.3 123.4 all-reduce.3
  1089.2 78.9 all-reduce.5
  1220.4 118.0 all-reduce.7
  1362.3 123.4 all-reduce.3
  1512.2 78.9 all-reduce.5
  1643.4 118.1 all-reduce.7
where the time goes:
time: 1800 us; the launch traced here: 1790 us
  waiting for transfers between devices  952 us (53%)
  blocking collectives  564 us (31%)
  other arithmetic  126 us (7%)
  local copies, waits for them, and re-layouts  76.4 us (4%)
  matrix products  49.5 us (3%)
    psum x12, waiting for transfers between devices, from_root(): return lax.psum(kept, axis)  952 us
    psum x4, blocking collectives, from_root(): return lax.psum(kept, axis)  500 us
    psum x1, blocking collectives, shards(): summed = lax.psum(partial_grad, ('frames', 'prow', 'pcol'))  64.5 us
    another operation x12, other arithmetic, eliminate(): factor_blk = jnp.linalg.cholesky(diag_blk)  49.9 us
    while x16, local copies, waits for them, and re-layouts  42.8 us
    another operation x8, other arithmetic, solve_rows(): jax.scipy.linalg.solve_triangular(factor_blk, right_side, lower=True)  42 us
  transfers between devices with their start and end apart: 12, of which 8 were waited for; matrix products, arithmetic and copies ran while one was open for 2% of the time, Pallas kernels for 0%

commit v1 on v0

v1 whole, which is shorter than its diff:
```python
import math

import jax
import jax.numpy as jnp
from jax import lax
from jax.experimental import pallas as pl
from jax.experimental.pallas import tpu as pltpu
from jax.sharding import PartitionSpec as P

NPAN = 8192
BS = 128
STEPS = 4
SHIFT = 2.5 * math.sqrt(NPAN)
PAIRS = [(k, m) for k in range(STEPS) for m in range(k + 1)]
NQ = len(PAIRS)
MESH = pl.DeviceIdType.MESH
precise = lax.Precision.HIGHEST
f32 = jnp.float32
bf16 = jnp.bfloat16
NT = (((1,), (1,)), ((), ()))


def loop(lo, hi, fn):
    def body(d, carry):
        fn(d)
        return carry

    lax.fori_loop(lo, hi, body, 0)


def exchange_kernel(
    mem, scand, ccand, pg,
    s_out, raw_r, raw_c, g_out,
    s1r, s1, s2r, par, mine, g1r, g1, g2r, g2, g3r,
    snd_s1, rcv_s1, snd_s2, rcv_s2, snd_s3, rcv_s3, snd_sx, rcv_sx,
    snd_a, rcv_a, snd_r, rcv_r, snd_t, rcv_t, snd_rx, rcv_rx, snd_cx, rcv_cx,
    snd_g1, rcv_g1, snd_g2, rcv_g2, snd_g3, rcv_g3, snd_g4, rcv_g4,
):
    f = lax.axis_index("frames")
    r = lax.axis_index("prow")
    c = lax.axis_index("pcol")

    def copy(src, dst, snd, rcv, f_to, r_to, c_to):
        return pltpu.make_async_remote_copy(
            src_ref=src, dst_ref=dst, send_sem=snd, recv_sem=rcv,
            device_id=(f_to, r_to, c_to), device_id_type=MESH,
        )

    def col_peer(d):
        return lax.rem(c + d, 8)

    def row_peer(d):
        return lax.rem(r + d, 8)

    def s1_copy(src, dst_slot, peer, sem):
        return copy(scand.at[src], s1r.at[dst_slot], snd_s1.at[peer], rcv_s1.at[sem], f, r, peer)

    def s1_send(d):
        peer = col_peer(d)
        s1_copy(peer + 8 * f, c, peer, c).start()

    loop(1, 8, s1_send)
    s1r[c] = scand[c + 8 * f]

    def g1_send(d):
        peer = col_peer(d)
        copy(pg.at[peer], g1r.at[c], snd_g1.at[peer], rcv_g1.at[c], f, r, peer).start()

    loop(1, 8, g1_send)
    g1r[c] = pg[c]

    def a_send(d):
        peer = col_peer(d)
        copy(ccand.at[peer, f], par.at[c], snd_a.at[peer], rcv_a.at[c], f, r, peer).start()

    loop(1, 8, a_send)
    par[c] = ccand[c, f]

    def s1_wait(d):
        peer = col_peer(d)
        s1_copy(peer + 8 * f, peer, peer, peer).wait()

    loop(1, 8, s1_wait)
    for q, (k, m) in enumerate(PAIRS):
        s1[q] = s1r[lax.rem(mem[m], 8), q]

    def s2_send(d):
        peer = row_peer(d)
        copy(s1, s2r.at[r], snd_s2.at[peer], rcv_s2.at[r], f, peer, c).start()

    loop(1, 8, s2_send)
    s2r[r] = s1[...]

    def g1_wait(d):
        peer = col_peer(d)
        copy(pg.at[peer], g1r.at[peer], snd_g1.at[peer], rcv_g1.at[peer], f, r, peer).wait()

    loop(1, 8, g1_wait)
    g1[...] = jnp.sum(g1r[...], axis=0)

    def g2_send(d):
        peer = row_peer(d)
        copy(g1, g2r.at[r], snd_g2.at[peer], rcv_g2.at[r], f, peer, c).start()

    loop(1, 8, g2_send)
    g2r[r] = g1[...]

    def s2_wait(d):
        peer = row_peer(d)
        copy(s1, s2r.at[peer], snd_s2.at[peer], rcv_s2.at[peer], f, peer, c).wait()

    loop(1, 8, s2_wait)
    here = c + 8 * f
    for q, (k, m) in enumerate(PAIRS):
        s_out[here, q] = s2r[lax.rem(mem[k], 8), q]

    def s3_send(d):
        peer = col_peer(d)
        copy(s_out.at[here], s_out.at[here], snd_s3.at[peer], rcv_s3.at[c], f, r, peer).start()

    loop(1, 8, s3_send)

    def sx_copy(slot, sem):
        return copy(s_out.at[slot], s_out.at[slot], snd_sx.at[sem], rcv_sx.at[sem], 1 - f, r, c)

    sx_copy(here, c).start()

    def s3_wait(d):
        peer = col_peer(d)
        slot = peer + 8 * f
        copy(s_out.at[slot], s_out.at[slot], snd_s3.at[peer], rcv_s3.at[peer], f, r, peer).wait_recv()
        sx_copy(slot, peer).start()

    loop(1, 8, s3_wait)

    def g2_wait(d):
        peer = row_peer(d)
        copy(g1, g2r.at[peer], snd_g2.at[peer], rcv_g2.at[peer], f, peer, c).wait()

    loop(1, 8, g2_wait)
    g2[...] = jnp.sum(g2r[...], axis=0)
    g3 = copy(g2, g3r, snd_g3, rcv_g3, 1 - f, r, c)
    g3.start()

    def a_wait(d):
        peer = col_peer(d)
        copy(ccand.at[peer, f], par.at[peer], snd_a.at[peer], rcv_a.at[peer], f, r, peer).wait()

    loop(1, 8, a_wait)
    for k in range(STEPS):
        mine[k] = par[lax.rem(mem[k], 8), k]

    def r_send(d):
        peer = col_peer(d)
        copy(mine, raw_r.at[c, f], snd_r.at[peer], rcv_r.at[c], f, r, peer).start()

    loop(1, 8, r_send)
    raw_r[c, f] = mine[...]

    def t_send(d):
        peer = row_peer(d)

        @pl.when(jnp.logical_or(peer != r, c != r))
        def _():
            copy(mine, raw_c.at[c, f], snd_t.at[peer], rcv_t.at[c], f, peer, r).start()

    loop(0, 8, t_send)

    @pl.when(r == c)
    def _():
        raw_c[c, f] = mine[...]

    g3.wait()
    g_out[c] = g2[...] + g3r[...]

    def g4_send(d):
        peer = col_peer(d)
        copy(g_out.at[c], g_out.at[c], snd_g4.at[peer], rcv_g4.at[c], f, r, peer).start()

    loop(1, 8, g4_send)

    def rx_copy(slot):
        return copy(raw_r.at[slot, f], raw_r.at[slot, f], snd_rx.at[slot], rcv_rx.at[slot], 1 - f, r, c)

    def cx_copy(slot):
        return copy(raw_c.at[slot, f], raw_c.at[slot, f], snd_cx.at[slot], rcv_cx.at[slot], 1 - f, r, c)

    rx_copy(c).start()

    def r_wait(d):
        peer = col_peer(d)
        copy(mine, raw_r.at[peer, f], snd_r.at[peer], rcv_r.at[peer], f, r, peer).wait_recv()
        rx_copy(peer).start()

    loop(1, 8, r_wait)

    def t_wait(b):
        @pl.when(jnp.logical_or(b != c, r != c))
        def _():
            copy(mine, raw_c.at[b, f], snd_t.at[b], rcv_t.at[b], f, c, b).wait_recv()

        cx_copy(b).start()

    loop(0, 8, t_wait)

    def g4_wait(d):
        peer = col_peer(d)
        copy(g_out.at[peer], g_out.at[peer], snd_g4.at[peer], rcv_g4.at[peer], f, r, peer).wait_recv()

    loop(1, 8, g4_wait)

    def x_wait(slot):
        other = 1 - f
        copy(s_out.at[slot + 8 * other], s_out.at[slot + 8 * other], snd_sx.at[slot], rcv_sx.at[slot], other, r, c).wait_recv()
        copy(raw_r.at[slot, other], raw_r.at[slot, other], snd_rx.at[slot], rcv_rx.at[slot], other, r, c).wait_recv()
        copy(raw_c.at[slot, other], raw_c.at[slot, other], snd_cx.at[slot], rcv_cx.at[slot], other, r, c).wait_recv()
        sx_copy(slot + 8 * f, slot).wait_send()
        rx_copy(slot).wait_send()
        cx_copy(slot).wait_send()

    loop(0, 8, x_wait)

    def tail(d):
        peer = col_peer(d)
        copy(s_out.at[here], s_out.at[here], snd_s3.at[peer], rcv_s3.at[c], f, r, peer).wait_send()
        copy(mine, raw_r.at[c, f], snd_r.at[peer], rcv_r.at[c], f, r, peer).wait_send()
        copy(g_out.at[c], g_out.at[c], snd_g4.at[peer], rcv_g4.at[c], f, r, peer).wait_send()

    loop(1, 8, tail)

    def t_tail(d):
        peer = row_peer(d)

        @pl.when(jnp.logical_or(peer != r, c != r))
        def _():
            copy(mine, raw_c.at[c, f], snd_t.at[peer], rcv_t.at[c], f, peer, r).wait_send()

    loop(0, 8, t_tail)


def exchange(mem, scand, ccand, pg):
    vm = pl.BlockSpec(memory_space=pltpu.VMEM)
    sem = pltpu.SemaphoreType.DMA
    return pl.pallas_call(
        exchange_kernel,
        out_shape=(
            jax.ShapeDtypeStruct((16, NQ, 8, BS), f32),
            jax.ShapeDtypeStruct((8, 2, STEPS, 64, BS), f32),
            jax.ShapeDtypeStruct((8, 2, STEPS, 64, BS), f32),
            jax.ShapeDtypeStruct((8, 8, BS), f32),
        ),
        in_specs=[pl.BlockSpec(memory_space=pltpu.SMEM), vm, vm, vm],
        out_specs=(vm, vm, vm, vm),
        scratch_shapes=[
            pltpu.VMEM((8, NQ, 8, BS), f32),
            pltpu.VMEM((NQ, 8, BS), f32),
            pltpu.VMEM((8, NQ, 8, BS), f32),
            pltpu.VMEM((8, STEPS, 64, BS), f32),
            pltpu.VMEM((STEPS, 64, BS), f32),
            pltpu.VMEM((8, 8, BS), f32),
            pltpu.VMEM((8, BS), f32),
            pltpu.VMEM((8, 8, BS), f32),
            pltpu.VMEM((8, BS), f32),
            pltpu.VMEM((8, BS), f32),
        ]
        + [sem((8,))] * 22
        + [sem, sem, sem((8,)), sem((8,))],
        compiler_params=pltpu.CompilerParams(has_side_effects=True, vmem_limit_bytes=40 << 20),
        name="exchange",
    )(mem, scand, ccand, pg)


def spread(row):
    return jnp.broadcast_to(row, (8, BS))


def factor_block(block):
    groups = BS // 8
    row_ids = lax.broadcasted_iota(jnp.int32, (8, BS), 0)
    lane_ids = lax.broadcasted_iota(jnp.int32, (8, BS), 1)
    upper = [block[8 * g : 8 * g + 8, :] for g in range(groups)]
    inv = [jnp.where(lane_ids == row_ids + 8 * g, 1.0, 0.0).astype(f32) for g in range(groups)]
    for g in range(groups):
        k = 8 * g
        v, w = upper[g], inv[g]
        cols = [jnp.broadcast_to(v[:, k + j : k + j + 1], (8, BS)) for j in range(8)]
        rows_v, rows_w, coef = [], [], []
        for j in range(8):
            pivot = spread(cols[j][j : j + 1, :])
            recip = 1.0 / pivot
            rv = spread(v[j : j + 1, :]) * recip
            rw = spread(w[j : j + 1, :]) * recip
            rows_v.append(rv)
            rows_w.append(rw)
            below = jnp.where(row_ids > j, cols[j], 0.0)
            coef.append([None] * 8)
            for t in range(j + 1, 8):
                coef[j][t] = spread(cols[t][j : j + 1, :]) * recip
                cols[t] = cols[t] - below * coef[j][t]
            v = v - below * rv
            w = w - below * rw
        upper[g], inv[g] = v, w
        for h in range(g + 1, groups):
            v, w = upper[h], inv[h]
            cols = [jnp.broadcast_to(v[:, k + j : k + j + 1], (8, BS)) for j in range(8)]
            for j in range(8):
                for t in range(j + 1, 8):
                    cols[t] = cols[t] - cols[j] * coef[j][t]
                v = v - cols[j] * rows_v[j]
                w = w - cols[j] * rows_w[j]
            upper[h], inv[h] = v, w
    full = jnp.concatenate(upper, axis=0)
    inverse = jnp.concatenate(inv, axis=0)
    rr = lax.broadcasted_iota(jnp.int32, (BS, BS), 0)
    cc = lax.broadcasted_iota(jnp.int32, (BS, BS), 1)
    pivots = jnp.sum(jnp.where(rr == cc, full, 0.0), axis=1, keepdims=True)
    scale = 1.0 / jnp.sqrt(pivots)
    return jnp.where(cc >= rr, full * scale, 0.0), inverse * scale


def dot_nt(a, b):
    return lax.dot_general(a, b, NT, precision=precise, preferred_element_type=f32)


def dot_nn(a, b):
    return lax.dot_general(a, b, (((1,), (0,)), ((), ())), precision=precise, preferred_element_type=f32)


def factor_kernel(mem, pat, s_ref, low_ref, inv_ref):
    rr = lax.broadcasted_iota(jnp.int32, (BS, BS), 0)
    cc = lax.broadcasted_iota(jnp.int32, (BS, BS), 1)
    low_ref[...] = jnp.zeros_like(low_ref)
    inv_ref[...] = jnp.zeros_like(inv_ref)

    def raw(k, m):
        q = PAIRS.index((k, m))
        keep = pat[mem[k], mem[m]].astype(f32)
        value = s_ref[:, q].reshape(BS, BS) * keep
        return value, keep

    for k in range(STEPS):
        lows = []
        for m in range(k):
            value, keep = raw(k, m)
            for t in range(m):
                value = value - keep * dot_nt(lows[t], low_ref[m, :, BS * t : BS * t + BS])
            lows.append(dot_nt(value, inv_ref[BS * m : BS * m + BS, BS * m : BS * m + BS]))
            low_ref[k, :, BS * m : BS * m + BS] = lows[m]
        value, _ = raw(k, k)
        value = value + jnp.where(rr == cc, SHIFT, 0.0)
        for t in range(k):
            value = value - dot_nt(lows[t], lows[t])
        upper, inverse = factor_block(value)
        low_ref[k, :, BS * k : BS * k + BS] = upper.T
        inv_ref[BS * k : BS * k + BS, BS * k : BS * k + BS] = inverse
        if k:
            row = jnp.concatenate(lows, axis=1)
            above = inv_ref[0 : BS * k, 0 : BS * k]
            inv_ref[BS * k : BS * k + BS, 0 : BS * k] = -dot_nn(inverse, dot_nn(row, above))


def factor(mem, pat, s):
    vm = pl.BlockSpec(memory_space=pltpu.VMEM)
    sm = pl.BlockSpec(memory_space=pltpu.SMEM)
    return pl.pallas_call(
        factor_kernel,
        out_shape=(
            jax.ShapeDtypeStruct((STEPS, BS, STEPS * BS), f32),
            jax.ShapeDtypeStruct((STEPS * BS, STEPS * BS), f32),
        ),
        in_specs=[sm, sm, vm],
        out_specs=(vm, vm),
        compiler_params=pltpu.CompilerParams(vmem_limit_bytes=40 << 20),
        name="factor",
    )(mem, pat, s)


def split(x):
    hi = x.astype(bf16)
    return hi, (x - hi.astype(f32)).astype(bf16)


def dot3(a, b):
    (ah, al), (bh, bl) = a, b
    d = lambda x, y: lax.dot_general(x, y, NT, preferred_element_type=f32)
    return d(ah, bh) + (d(ah, bl) + d(al, bh))


def update_kernel(
    where, mem, pat, low_ref, inv_ref, raw_r, raw_c, g_ref, hess, out, grad_out,
    blocks, xr, xr_hi, xr_lo, xc_hi, xc_lo, wh, wl, in_sem, out_sem,
):
    r, c = where[0], where[1]
    half = SNW = 2 * BS

    def load(b):
        return pltpu.make_async_copy(hess.at[:, :, b, :, :], blocks.at[b], in_sem.at[b])

    for b in range(8):
        load(b).start()

    h, l = split(inv_ref[...])
    wh[...] = h
    wl[...] = l
    w11 = (wh[0:SNW, 0:SNW], wl[0:SNW, 0:SNW])
    w21 = (wh[SNW:, 0:SNW], wl[SNW:, 0:SNW])
    w22 = (wh[SNW:, SNW:], wl[SNW:, SNW:])

    def keeps(i):
        pivot = i == mem[0]
        for k in range(1, STEPS):
            pivot = jnp.logical_or(pivot, i == mem[k])
        z = jnp.where(pivot, 0.0, 1.0).astype(f32)
        return z * pat[i, mem[0]].astype(f32), z * pat[i, mem[2]].astype(f32), z

    def panel(raw, base, store):
        for a in range(8):
            m1, m2, _ = keeps(8 * a + base)
            one = jnp.concatenate([raw[a, :, k].reshape(BS, BS) for k in (0, 1)], axis=1) * m1
            two = jnp.concatenate([raw[a, :, k].reshape(BS, BS) for k in (2, 3)], axis=1)
            one = split(one)
            x1 = dot3(one, w11)
            x2 = m2 * (dot3(one, w21) + dot3(split(two), w22))
            store(a, x1, x2)

    def store_r(a, x1, x2):
        rows = slice(BS * a, BS * a + BS)
        for lo, x in ((0, x1), (SNW, x2)):
            xr[rows, lo : lo + SNW] = x
            h, l = split(x)
            xr_hi[rows, lo : lo + SNW] = h
            xr_lo[rows, lo : lo + SNW] = l

    def store_c(a, x1, x2):
        rows = slice(BS * a, BS * a + BS)
        for lo, x in ((0, x1), (SNW, x2)):
            h, l = split(x)
            xc_hi[rows, lo : lo + SNW] = h
            xc_lo[rows, lo : lo + SNW] = l

    panel(raw_r, r, store_r)
    panel(raw_c, c, store_c)

    gp = jnp.concatenate(
        [g_ref[mem[k] // 8, pl.ds(lax.rem(mem[k], 8), 1), :] for k in range(STEPS)], axis=1
    )
    gp = jnp.broadcast_to(gp, (16, STEPS * BS))
    y = dot3(split(gp), (wh[...], wl[...]))
    dec = dot3(split(y), (xr_hi[...], xr_lo[...]))
    for a in range(8):
        i = 8 * a + r
        val = g_ref[a, pl.ds(r, 1), :] - dec[0:1, BS * a : BS * a + BS]
        for k in range(STEPS):
            val = jnp.where(i == mem[k], y[0:1, BS * k : BS * k + BS], val)
        grad_out[a : a + 1, :] = val

    rr = lax.broadcasted_iota(jnp.int32, (BS, BS), 0)
    cc = lax.broadcasted_iota(jnp.int32, (BS, BS), 1)
    shift = jnp.where(rr == cc, SHIFT, 0.0)
    xr_pair = (xr_hi[...], xr_lo[...])
    for bp in range(4):
        cols = slice(SNW * bp, SNW * bp + SNW)
        upd = dot3(xr_pair, (xc_hi[cols, :], xc_lo[cols, :]))
        for half in range(2):
            b = 2 * bp + half
            j = 8 * b + c
            load(b).wait()
            for a in range(8):
                i = 8 * a + r
                _, _, z = keeps(i)
                keep = z * pat[i, j].astype(f32)
                on = jnp.where(i == j, 1.0, 0.0).astype(f32) * z
                sub = upd[BS * a : BS * a + BS, BS * half : BS * half + BS]
                old = blocks[b, a].reshape(BS, BS)
                blocks[b, a] = (keep * (old - sub) + on * shift).reshape(BS, 1, BS)
            for k in range(STEPS):
                @pl.when(j == mem[k])
                def _():
                    for a in range(8):
                        blocks[b, a] = xr[BS * a : BS * a + BS, BS * k : BS * k + BS].reshape(BS, 1, BS)

                    @pl.when(lax.rem(mem[k], 8) == r)
                    def _():
                        blocks[b, mem[k] // 8] = low_ref[k, :, BS * k : BS * k + BS].reshape(BS, 1, BS)
            pltpu.make_async_copy(blocks.at[b], out.at[:, :, b, :, :], out_sem.at[b]).start()
    for b in range(8):
        pltpu.make_async_copy(blocks.at[b], out.at[:, :, b, :, :], out_sem.at[b]).wait()


def update(where, mem, pat, low, inv, raw_r, raw_c, g, hess):
    vm = pl.BlockSpec(memory_space=pltpu.VMEM)
    sm = pl.BlockSpec(memory_space=pltpu.SMEM)
    anywhere = pl.BlockSpec(memory_space=pl.ANY)
    wide = STEPS * BS
    return pl.pallas_call(
        update_kernel,
        out_shape=(
            jax.ShapeDtypeStruct(hess.shape, f32),
            jax.ShapeDtypeStruct((8, BS), f32),
        ),
        in_specs=[sm, sm, sm, vm, vm, vm, vm, vm, anywhere],
        out_specs=(anywhere, vm),
        scratch_shapes=[
            pltpu.VMEM((8, 8, BS, 1, BS), f32),
            pltpu.VMEM((1024, wide), f32),
            pltpu.VMEM((1024, wide), bf16),
            pltpu.VMEM((1024, wide), bf16),
            pltpu.VMEM((1024, wide), bf16),
            pltpu.VMEM((1024, wide), bf16),
            pltpu.VMEM((wide, wide), bf16),
            pltpu.VMEM((wide, wide), bf16),
            pltpu.SemaphoreType.DMA((8,)),
            pltpu.SemaphoreType.DMA((8,)),
        ],
        compiler_params=pltpu.CompilerParams(vmem_limit_bytes=48 << 20),
        name="update",
    )(where, mem, pat, low, inv, raw_r, raw_c, g, hess)


def shards(
    poses, codebook, offsets, confidence, code_ids, creature_ids, hess_raw, pattern, membership
):
    frame_total = poses.shape[0] * 128
    code_count = codebook.shape[0]
    kind_count = offsets.shape[0]
    mem = membership.reshape(-1)
    code_table = (code_ids[None, :] == jnp.arange(code_count, dtype=jnp.int32)[:, None]).astype(f32)
    kind_table = (creature_ids[None, :] == jnp.arange(kind_count, dtype=jnp.int32)[:, None]).astype(f32)
    predicted = jnp.einsum("cf,cw->fw", code_table, codebook.astype(f32), precision=precise)
    predicted = predicted + jnp.einsum("cf,cw->fw", kind_table, offsets.astype(f32), precision=precise)
    residual = confidence[:, None] * (poses.astype(f32) - predicted)
    pg = jnp.einsum("cf,fw->cw", code_table, residual, precision=precise) / math.sqrt(frame_total / code_count)
    pg = pg.reshape(8, 8, BS)

    hess = hess_raw.reshape(8, BS, 8, BS)
    slot = mem // 8
    ccand = jnp.stack([lax.dynamic_index_in_dim(hess, slot[k], 2, False) for k in range(STEPS)], axis=1)
    ccand = ccand.reshape(8, STEPS, 2, 64, BS).transpose(0, 2, 1, 3, 4)
    scand = jnp.stack(
        [
            lax.dynamic_slice(hess, (slot[k], 0, slot[m], 0), (1, BS, 1, BS)).reshape(16, 8, BS)
            for k, m in PAIRS
        ],
        axis=1,
    )
    s, raw_r, raw_c, g = exchange(mem, scand, ccand, pg)
    low, inv = factor(mem, pattern, s)
    where = jnp.stack([lax.axis_index("prow"), lax.axis_index("pcol")]).astype(jnp.int32)
    state, grad = update(
        where, mem, pattern, low, inv, raw_r, raw_c, g, hess_raw.reshape(8, BS, 8, 1, BS)
    )
    return state.reshape(hess_raw.shape), grad.reshape(8, 1, BS)


def solution(mesh):
    return jax.shard_map(
        shards,
        mesh=mesh,
        in_specs=(
            P(("frames", "prow", "pcol"), None),
            P(),
            P(),
            P(("frames", "prow", "pcol")),
            P(("frames", "prow", "pcol")),
            P(("frames", "prow", "pcol")),
            P(None, "prow", None, None, "pcol", None),
            P(),
            P(),
        ),
        out_specs=(P(None, "prow", None, None, "pcol", None), P(None, "prow", None)),
        check_vma=False,
    )
```

time: 1800 us -> 154 us (0.09)
  the two profiles are of different devices: /device:TPU:105 before, /device:TPU:97 now
where the time goes in v1:
time: 154 us; the launch traced here: 151 us
  Pallas kernels  133 us (86%)
  between operations  8.58 us (6%)
  local copies, waits for them, and re-layouts  6.88 us (4%)
  matrix products  2.24 us (1%)
    pallas_call x1, Pallas kernels, exchange(): pl.pallas_call(exchange_kernel, out_shape=(jax.ShapeDtypeStruct((16, NQ,...  89 us
    pallas_call x1, Pallas kernels, update(): pl.pallas_call(update_kernel, out_shape=(jax.ShapeDtypeStruct(hess.shape,...  22.6 us
    pallas_call x1, Pallas kernels, factor(): pl.pallas_call(factor_kernel, out_shape=(jax.ShapeDtypeStruct((STEPS, BS,...  21.4 us

profile of v1, /device:TPU:97, one launch (start us, length us, event | category | flops | bytes accessed | tf_op | source)
XLA Modules:
  0.0 151.0 jit_solution(384372061599509790)
XLA Ops:
  0.6 0.0 copy-start
  0.6 0.1 pad_add_fusion.where
  0.7 0.8 reshape.64.mem
  1.5 0.6 fusion.6
  9.5 1.2 constant_dynamic-slice_fusion.4
  10.9 1.7 %constant_dynamic-slice_fusion.3 = (f32[8,1,128,1,1,128]{5,4,3,2,1,0:T(1,128)S(1)}, f32[8,1,128,1,1,128]{5,4,3,2,1,0:T(1,128)S(1)}, f32[8,1,128,1,1,128]{5,4,3,2,1,0:T(1,128)S(1)}, f32[8,1,128,1,1,128]{5,4,3,2,1,0:T(1,128)S(1)}) fusion(f32[8,1,128,8,1,128]{5,4,3,2,1,0:T(1,128)} %param.15, s32[]{:T(128)S(6)} %select_n.19, s32[]{:T(128)S(6)} %select_n.21, ...), kind=kLoop, calls=%fused_computation.24 | loop fusion | bytes 4194320 | tf_op jit(solution)/shard_map/jit(dynamic_index_in_dim)/dynamic_slice | solution.py:537
  12.6 0.0 copy-start.4
  12.6 0.1 maximum_bitcast_fusion.ccand
  12.7 0.0 copy-done
  12.7 0.5 copy-done.4
  13.3 0.0 copy-start.3
  13.3 0.0 copy-start.5
  13.3 0.0 copy-start.6
  13.3 0.0 copy-start.7
  13.3 0.5 fusion.2
  13.8 0.7 copy-done.3
  14.5 0.0 copy-done.5
  14.5 0.0 copy-done.6
  14.5 0.0 copy-done.7
  14.5 0.9 fusion.1
  15.4 0.0 copy-start.2
  15.4 0.9 convolution_multiply_fusion
  16.3 89.0 %exchange.1 = (f32[16,10,8,128]{3,2,1,0:T(8,128)S(1)}, f32[8,2,4,64,128]{4,3,2,1,0:T(8,128)S(1)}, f32[8,2,4,64,128]{4,3,2,1,0:T(8,128)S(1)}, f32[8,8,128]{2,1,0:T(8,128)S(1)}) custom-call(s32[4]{0:T(128)S(1)} %reshape.64.mem, f32[16,10,8,128]{3,2,1,0:T(8,128)S(1)} %constant_dynamic-update-slice_fusion.scand, ...), custom_call_target="tpu_custom_call" | custom-call | tf_op jit(solution)/shard_map/exchange/pallas_call | solution.py:244
  105.3 0.0 copy-start.1
  105.3 1.3 copy-done.1
  106.6 0.0 copy-done.2
  106.6 21.4 %factor.1 = (f32[4,128,512]{2,1,0:T(8,128)S(1)}, f32[512,512]{1,0:T(8,128)S(1)}) custom-call(s32[4]{0:T(128)S(1)} %reshape.64.mem, s32[64,64]{1,0:T(8,128)S(1)} %copy-done.2, f32[16,10,8,128]{3,2,1,0:T(8,128)S(1)} %get-tuple-element.10.s_ref), custom_call_target="tpu_custom_call" | custom-call | tf_op jit(solution)/shard_map/factor/pallas_call | solution.py:365
  128.1 22.6 %update.1 = (f32[8,128,8,1,128]{4,3,2,1,0:T(1,128)}, f32[8,128]{1,0:T(8,128)}) custom-call(s32[2]{0:T(128)S(1)} %pad_add_fusion.where, s32[4]{0:T(128)S(1)} %reshape.64.mem, s32[64,64]{1,0:T(8,128)S(1)} %copy-done.2, f32[4,128,512]{2,1,0:T(8,128)S(1)} %get-tuple-element.11.low_ref, f32[512,512]{1,0:T(8,128)S(1)} %get-tuple-element.12.inv_ref, ...), custom_call_target="tpu_custom_call" | custom-call | tf_op jit(solution)/shard_map/update/pallas_call | solution.py:495
  (12 shorter events, 0.1 us)
Async XLA Ops:
  0.6 12.1 %copy-start = (bf16[32,256]{1,0:T(8,128)(2,1)S(1)}, bf16[32,256]{1,0:T(8,128)(2,1)}, u32[]{:S(2)}) copy-start(bf16[32,256]{1,0:T(8,128)(2,1)} %param.10) | copy-start | bytes 49156
  12.6 0.7 copy-start.4
  13.3 1.2 copy-start.3
  13.3 1.2 copy-start.5
  13.3 1.2 copy-start.6
  13.3 1.2 copy-start.7
  15.4 91.2 %copy-start.2 = (s32[64,64]{1,0:T(8,128)S(1)}, s32[64,64]{1,0:T(8,128)}, u32[]{:S(2)}) copy-start(s32[64,64]{1,0:T(8,128)} %pat.3) | copy-start | bytes 49156
  105.3 1.3 copy-start.1

commit v2 on v0

v2 whole, which is shorter than its diff:
```python
import math

import jax
import jax.numpy as jnp
from jax import lax
from jax.experimental import pallas as pl
from jax.experimental.pallas import tpu as pltpu
from jax.sharding import PartitionSpec as P

NPAN = 8192
BS = 128
STEPS = 4
FRAMES = 262144
CODES = 32
SHIFT = 2.5 * math.sqrt(NPAN)
PAIRS = [(k, m) for k in range(STEPS) for m in range(k + 1)]
NQ = len(PAIRS)
CHUNKS = ((0, 3), (3, 7))
WIDE = STEPS * BS
MESH = pl.DeviceIdType.MESH
precise = lax.Precision.HIGHEST
f32 = jnp.float32
bf16 = jnp.bfloat16
NT = (((1,), (1,)), ((), ()))
NN = (((1,), (0,)), ((), ()))


def loop(lo, hi, fn):
    def body(d, carry):
        fn(d)
        return carry

    lax.fori_loop(lo, hi, body, 0)


def split(x):
    hi = x.astype(bf16)
    return hi, (x - hi.astype(f32)).astype(bf16)


def dot3(a, b):
    (ah, al), (bh, bl) = a, b
    d = lambda x, y: lax.dot_general(x, y, NT, preferred_element_type=f32)
    return d(ah, bh) + (d(ah, bl) + d(al, bh))


def member(mem, k):
    return mem[k // 2, k % 2]


VM = pl.BlockSpec(memory_space=pltpu.VMEM)
SM = pl.BlockSpec(memory_space=pltpu.SMEM)
ANY = pl.BlockSpec(memory_space=pl.ANY)


def prepare_kernel(mem, hess, poses, codebook, offsets, conf, codes, kinds, scand, ccand, pg, sem):
    f = lax.axis_index("frames")
    slot = [member(mem, k) // 8 for k in range(STEPS)]
    copies = [
        pltpu.make_async_copy(hess.at[slot[k], :, slot[m], 0, :], scand.at[q], sem.at[q])
        for q, (k, m) in enumerate(PAIRS)
    ]
    for copy in copies:
        copy.start()
    by_col = [
        pltpu.make_async_copy(hess.at[:, :, slot[k], 0, :], ccand.at[:, k], sem.at[NQ + k])
        for k in range(2)
    ]
    by_row = [
        pltpu.make_async_copy(hess.at[slot[2 + k], :, b, 0, :], ccand.at[b, k], sem.at[NQ + 2 + 8 * k + b])
        for k in range(2)
        for b in range(8)
    ]

    @pl.when(f == 0)
    def _():
        for copy in by_col:
            copy.start()

    @pl.when(f == 1)
    def _():
        for copy in by_row:
            copy.start()

    ids = lax.broadcasted_iota(jnp.int32, (CODES, BS), 0)
    weights, marks = [], []
    for s in range(16):
        weights.append(jnp.where(codes[s : s + 1, :] == ids, conf[s : s + 1, :], 0.0))
        marks.append(jnp.where(kinds[s : s + 1, :] == ids, 1.0, 0.0).astype(bf16))
    weight = jnp.concatenate(weights, axis=1)
    mark = jnp.concatenate(marks, axis=1)
    parts = []
    for _ in range(3):
        parts.append(weight.astype(bf16))
        weight = weight - parts[-1].astype(f32)
    stack = jnp.concatenate(parts, axis=0)

    def total(x):
        return x[0:CODES] + (x[CODES : 2 * CODES] + x[2 * CODES : 3 * CODES])

    moment = total(lax.dot_general(stack, poses[...], NN, preferred_element_type=f32))
    pair = total(lax.dot_general(stack, mark, NT, preferred_element_type=f32))
    count = jnp.sum(pair, axis=1, keepdims=True)
    moment = moment - count * codebook[...].astype(f32)
    moment = moment - lax.dot_general(
        pair, offsets[...].astype(f32), NN, precision=precise, preferred_element_type=f32
    )
    moment = moment / math.sqrt(FRAMES / CODES)
    for half in range(2):
        pg[pl.ds(half, CODES, stride=2), :] = moment[:, BS * half : BS * half + BS]

    for copy in copies:
        copy.wait()

    @pl.when(f == 0)
    def _():
        for copy in by_col:
            copy.wait()

    @pl.when(f == 1)
    def _():
        for copy in by_row:
            copy.wait()


def prepare(mem, hess, poses, codebook, offsets, conf, codes, kinds):
    return pl.pallas_call(
        prepare_kernel,
        out_shape=(
            jax.ShapeDtypeStruct((NQ, BS, BS), f32),
            jax.ShapeDtypeStruct((8, 2, BS, BS), f32),
            jax.ShapeDtypeStruct((64, BS), f32),
        ),
        in_specs=[SM, ANY, VM, VM, VM, VM, VM, VM],
        out_specs=(VM, VM, VM),
        scratch_shapes=[pltpu.SemaphoreType.DMA((NQ + 18,))],
        compiler_params=pltpu.CompilerParams(vmem_limit_bytes=24 << 20),
        name="prepare",
    )(mem, hess, poses, codebook, offsets, conf, codes, kinds)


def spread(row):
    return jnp.broadcast_to(row, (8, BS))


def factor_block(block):
    groups = BS // 8
    row_ids = lax.broadcasted_iota(jnp.int32, (8, BS), 0)
    lane_ids = lax.broadcasted_iota(jnp.int32, (8, BS), 1)
    upper = [block[8 * g : 8 * g + 8, :] for g in range(groups)]
    inv = [jnp.where(lane_ids == row_ids + 8 * g, 1.0, 0.0).astype(f32) for g in range(groups)]
    for g in range(groups):
        k = 8 * g
        v, w = upper[g], inv[g]
        cols = [jnp.broadcast_to(v[:, k + j : k + j + 1], (8, BS)) for j in range(8)]
        rows_v, rows_w, coef = [], [], []
        for j in range(8):
            pivot = spread(cols[j][j : j + 1, :])
            recip = 1.0 / pivot
            rv = spread(v[j : j + 1, :]) * recip
            rw = spread(w[j : j + 1, :]) * recip
            rows_v.append(rv)
            rows_w.append(rw)
            below = jnp.where(row_ids > j, cols[j], 0.0)
            coef.append([None] * 8)
            for t in range(j + 1, 8):
                coef[j][t] = spread(cols[t][j : j + 1, :]) * recip
                cols[t] = cols[t] - below * coef[j][t]
            v = v - below * rv
            w = w - below * rw
        upper[g], inv[g] = v, w
        for h in range(g + 1, groups):
            v, w = upper[h], inv[h]
            cols = [jnp.broadcast_to(v[:, k + j : k + j + 1], (8, BS)) for j in range(8)]
            for j in range(8):
                for t in range(j + 1, 8):
                    cols[t] = cols[t] - cols[j] * coef[j][t]
                v = v - cols[j] * rows_v[j]
                w = w - cols[j] * rows_w[j]
            upper[h], inv[h] = v, w
    full = jnp.concatenate(upper, axis=0)
    inverse = jnp.concatenate(inv, axis=0)
    rr = lax.broadcasted_iota(jnp.int32, (BS, BS), 0)
    cc = lax.broadcasted_iota(jnp.int32, (BS, BS), 1)
    pivots = jnp.sum(jnp.where(rr == cc, full, 0.0), axis=1, keepdims=True)
    scale = 1.0 / jnp.sqrt(pivots)
    return jnp.where(cc >= rr, full * scale, 0.0), inverse * scale


def dot_nt(a, b):
    return lax.dot_general(a, b, NT, precision=precise, preferred_element_type=f32)


def dot_nn(a, b):
    return lax.dot_general(a, b, (((1,), (0,)), ((), ())), precision=precise, preferred_element_type=f32)


def exchange_kernel(
    mem, pat, scand, ccand, pg,
    x_hi, x_lo, diag, y_out, g_out,
    s_all, low, inv, cur, fac_u, fac_i, raw, wh, wl,
    s1r_a, s1r_b, s1, s2r_a, s2r_b, par, mine, g1r, g1, g2r, g2, g3r,
    snd_s1, rcv_s1, snd_s2, rcv_s2, snd_s3, rcv_s3, snd_sx, rcv_sx,
    snd_a, rcv_a, snd_r, rcv_r, snd_t, rcv_t, snd_x, rcv_x,
    snd_g1, rcv_g1, snd_g2, rcv_g2, snd_g4, rcv_g4, snd_g3, rcv_g3,
):
    s1r, s2r = (s1r_a, s1r_b), (s2r_a, s2r_b)
    f = lax.axis_index("frames")
    r = lax.axis_index("prow")
    c = lax.axis_index("pcol")
    p = r + f * (c - r)
    q = c + f * (r - c)

    def place(p_to, q_to):
        return (f, p_to + f * (q_to - p_to), q_to + f * (p_to - q_to))

    sibling = (1 - f, r, c)

    def copy(src, dst, snd, rcv, to):
        return pltpu.make_async_remote_copy(
            src_ref=src, dst_ref=dst, send_sem=snd, recv_sem=rcv, device_id=to, device_id_type=MESH
        )

    def q_peer(d):
        return lax.rem(q + d, 8)

    def p_peer(d):
        return lax.rem(p + d, 8)

    def c_peer(d):
        return lax.rem(c + d, 8)

    def r_peer(d):
        return lax.rem(r + d, 8)

    barrier = pltpu.get_barrier_semaphore()

    def greet(to):
        pl.semaphore_signal(barrier, inc=1, device_id=to, device_id_type=MESH)

    greet(sibling)

    def greet_line(d):
        greet(place(p, q_peer(d)))
        greet(place(p_peer(d), q))

    loop(1, 8, greet_line)

    def greet_turn(d):
        @pl.when(jnp.logical_or(d != p, p != q))
        def _():
            greet(place(d, p))

        @pl.when(jnp.logical_or(d != q, p != q))
        def _():
            greet(place(q, d))

    loop(0, 8, greet_turn)
    same = jnp.where(p == q, 1, 0)
    pl.semaphore_wait(barrier, 31 - 2 * same)

    def rows_of(slice_id):
        return pl.ds(pl.multiple_of(8 * slice_id, 8), 8)

    def s1_copy(h, peer, at):
        lo, n = CHUNKS[h]
        return copy(
            scand.at[pl.ds(lo, n), rows_of(peer + 8 * f), :], s1r[h].at[at],
            snd_s1.at[h, peer], rcv_s1.at[h, at], place(p, peer),
        )

    def s2_copy(h, peer, at):
        lo, n = CHUNKS[h]
        return copy(
            s1.at[pl.ds(lo, n)], s2r[h].at[at],
            snd_s2.at[h, peer], rcv_s2.at[h, at], place(peer, q),
        )

    def s3_copy(h, peer, at):
        lo, n = CHUNKS[h]
        part = s_all.at[pl.ds(lo, n), rows_of(at + 8 * f), :]
        return copy(part, part, snd_s3.at[h, peer], rcv_s3.at[h, at], place(p, peer))

    def sx_copy(h, at, core):
        lo, n = CHUNKS[h]
        part = s_all.at[pl.ds(lo, n), rows_of(at + 8 * core), :]
        return copy(part, part, snd_sx.at[h, at], rcv_sx.at[h, at], sibling)

    def g1_copy(peer, at):
        return copy(pg.at[peer], g1r.at[at], snd_g1.at[peer], rcv_g1.at[at], (f, r, peer))

    def g2_copy(peer, at):
        return copy(g1, g2r.at[at], snd_g2.at[peer], rcv_g2.at[at], (f, peer, c))

    def g4_copy(peer, at):
        return copy(g_out.at[at], g_out.at[at], snd_g4.at[peer], rcv_g4.at[at], (f, r, peer))

    def a_copy(peer, at):
        return copy(ccand.at[peer], par.at[at], snd_a.at[peer], rcv_a.at[at], place(p, peer))

    def r_copy(peer, at):
        return copy(mine, raw.at[f, f, at], snd_r.at[peer], rcv_r.at[at], place(p, peer))

    def t_copy(peer, at):
        return copy(mine, raw.at[1 - f, f, at], snd_t.at[peer], rcv_t.at[at], place(peer, p))

    def x_copy(which, at, core):
        part = raw.at[which, core, at]
        return copy(part, part, snd_x.at[which, at], rcv_x.at[which, at], sibling)

    for h in range(2):
        loop(1, 8, lambda d: s1_copy(h, q_peer(d), q).start())
    loop(1, 8, lambda d: g1_copy(c_peer(d), c).start())
    for h, (lo, n) in enumerate(CHUNKS):
        s1r[h][q] = scand[lo : lo + n, rows_of(q + 8 * f), :]
    g1r[c] = pg[c]
    par[q] = ccand[q]

    for h in range(2):
        lo, n = CHUNKS[h]
        loop(1, 8, lambda d: s1_copy(h, q_peer(d), q_peer(d)).wait())
        for e in range(lo, lo + n):
            own_k = lax.rem(member(mem, PAIRS[e][0]), 8)
            own_m = lax.rem(member(mem, PAIRS[e][1]), 8)
            s1[e] = s1r[h][own_m + f * (own_k - own_m), e - lo]
        loop(1, 8, lambda d: s2_copy(h, p_peer(d), p).start())
        s2r[h][p] = s1[lo : lo + n]

    loop(1, 8, lambda d: g1_copy(c_peer(d), c_peer(d)).wait())
    g1[...] = jnp.sum(g1r[...], axis=0)
    loop(1, 8, lambda d: g2_copy(r_peer(d), r).start())
    g2r[r] = g1[...]


    for h in range(2):
        lo, n = CHUNKS[h]
        loop(1, 8, lambda d: s2_copy(h, p_peer(d), p_peer(d)).wait())
        for e in range(lo, lo + n):
            own_k = lax.rem(member(mem, PAIRS[e][0]), 8)
            own_m = lax.rem(member(mem, PAIRS[e][1]), 8)
            s_all[e, rows_of(q + 8 * f), :] = s2r[h][own_k + f * (own_m - own_k), e - lo]
        loop(1, 8, lambda d: s3_copy(h, q_peer(d), q).start())
        sx_copy(h, q, f).start()

    loop(1, 8, lambda d: a_copy(q_peer(d), q).start())

    loop(1, 8, lambda d: g2_copy(r_peer(d), r_peer(d)).wait())
    g2[...] = jnp.sum(g2r[...], axis=0)
    g3 = copy(g2, g3r, snd_g3, rcv_g3, sibling)
    g3.start()

    def pass_on(h):
        def one(d):
            s3_copy(h, q_peer(d), q_peer(d)).wait_recv()
            sx_copy(h, q_peer(d), f).start()

        loop(1, 8, one)

    def sx_ready(h):
        loop(0, 8, lambda at: sx_copy(h, at, 1 - f).wait_recv())

    pass_on(0)

    rr = lax.broadcasted_iota(jnp.int32, (BS, BS), 0)
    cc = lax.broadcasted_iota(jnp.int32, (BS, BS), 1)
    low[...] = jnp.zeros_like(low)
    inv[...] = jnp.zeros_like(inv)

    def before(k):
        if k == 0:
            sx_ready(0)
        if k == 2:
            sx_ready(1)
        for m in range(k):
            keep = pat[member(mem, k), member(mem, m)].astype(f32)
            value = s_all[PAIRS.index((k, m))] * keep
            if m:
                value = value - keep * dot_nt(low[k, :, 0 : BS * m], low[m, :, 0 : BS * m])
            low[k, :, BS * m : BS * m + BS] = dot_nt(value, inv[BS * m : BS * m + BS, BS * m : BS * m + BS])
        value = s_all[PAIRS.index((k, k))] * pat[member(mem, k), member(mem, k)].astype(f32)
        value = value + jnp.where(rr == cc, SHIFT, 0.0)
        if k:
            lows = low[k, :, 0 : BS * k]
            value = value - dot_nt(lows, lows)
        cur[...] = value

    def after(k):
        at = slice(BS * k, BS * k + BS)
        inv[at, at] = fac_i[...]
        if k:
            inv[at, 0 : BS * k] = -dot_nn(fac_i[...], dot_nn(low[k, :, 0 : BS * k], inv[0 : BS * k, 0 : BS * k]))
        lower = fac_u[...].T
        low[k, :, at] = lower
        diag[k] = lower
        if k == 0:
            pass_on(1)
        if k == 1:
            spread_panels()
        if k == 2:
            g3.wait()
            g_out[c] = g2[...] + g3r[...]
            loop(1, 8, lambda d: g4_copy(c_peer(d), c).start())

    def spread_panels():
        loop(1, 8, lambda d: a_copy(q_peer(d), q_peer(d)).wait())

        @pl.when(f == 0)
        def _():
            for k in range(2):
                mine[k] = par[lax.rem(mem[0, k], 8), k]

        @pl.when(f == 1)
        def _():
            for k in range(2):
                mine[k] = par[lax.rem(mem[1, k], 8), k].T

        loop(1, 8, lambda d: r_copy(q_peer(d), q).start())
        raw[f, f, q] = mine[...]

        def turn(d):
            @pl.when(jnp.logical_or(d != p, p != q))
            def _():
                t_copy(d, q).start()

        loop(0, 8, turn)

        @pl.when(p == q)
        def _():
            raw[1 - f, f, q] = mine[...]

        x_copy(f, q, f).start()

    def step(k):
        for kk in range(STEPS):
            @pl.when(k == kk)
            def _():
                before(kk)

        upper, inverse = factor_block(cur[...])
        fac_u[...] = upper
        fac_i[...] = inverse
        for kk in range(STEPS):
            @pl.when(k == kk)
            def _():
                after(kk)

    loop(0, STEPS, step)

    def r_arrives(d):
        r_copy(q_peer(d), q_peer(d)).wait_recv()
        x_copy(f, q_peer(d), f).start()

    loop(1, 8, r_arrives)

    def t_arrives(b):
        @pl.when(jnp.logical_or(b != q, p != q))
        def _():
            t_copy(b, b).wait_recv()

        x_copy(1 - f, b, f).start()

    loop(0, 8, t_arrives)

    h, l = split(inv[...])
    wh[...] = h
    wl[...] = l
    half = 2 * BS
    w11 = (wh[0:half, 0:half], wl[0:half, 0:half])
    w21 = (wh[half:, 0:half], wl[half:, 0:half])
    w22 = (wh[half:, half:], wl[half:, half:])

    loop(1, 8, lambda d: g4_copy(c_peer(d), c_peer(d)).wait_recv())
    gp = jnp.concatenate(
        [g_out[member(mem, k) // 8, pl.ds(lax.rem(member(mem, k), 8), 1), :] for k in range(STEPS)], axis=1
    )
    gp = jnp.broadcast_to(gp, (16, WIDE))
    y_out[...] = dot3(split(gp), (wh[...], wl[...]))[0:8]

    def panel(which, a):
        base = r + which * (c - r)
        i = 8 * a + base
        pivot = i == member(mem, 0)
        for k in range(1, STEPS):
            pivot = jnp.logical_or(pivot, i == member(mem, k))
        z = jnp.where(pivot, 0.0, 1.0).astype(f32)
        m1 = z * pat[i, member(mem, 0)].astype(f32)
        m2 = z * pat[i, member(mem, 2)].astype(f32)
        one = split(jnp.concatenate([raw[which, 0, a, 0], raw[which, 0, a, 1]], axis=1) * m1)
        two = split(jnp.concatenate([raw[which, 1, a, 0], raw[which, 1, a, 1]], axis=1))
        rows = pl.ds(pl.multiple_of(BS * a, BS), BS)
        for lo, x in ((0, dot3(one, w11)), (half, m2 * (dot3(one, w21) + dot3(two, w22)))):
            hi, rest = split(x)
            x_hi[which, rows, lo : lo + half] = hi
            x_lo[which, rows, lo : lo + half] = rest

    def panel_step(t):
        which = t // 8
        a = lax.rem(t, 8)
        x_copy(which, a, 1 - f).wait_recv()
        panel(which, a)

    loop(0, 16, panel_step)

    def tail(d):
        for h in range(2):
            s3_copy(h, q_peer(d), q).wait_send()
        r_copy(q_peer(d), q).wait_send()
        g4_copy(c_peer(d), c).wait_send()

    loop(1, 8, tail)

    def tail_turn(d):
        @pl.when(jnp.logical_or(d != p, p != q))
        def _():
            t_copy(d, q).wait_send()

        for h in range(2):
            sx_copy(h, d, f).wait_send()
        for which in range(2):
            x_copy(which, d, f).wait_send()

    loop(0, 8, tail_turn)


def exchange(mem, pat, scand, ccand, pg):
    vmem = pltpu.VMEM
    sem = pltpu.SemaphoreType.DMA
    return pl.pallas_call(
        exchange_kernel,
        out_shape=(
            jax.ShapeDtypeStruct((2, 1024, WIDE), bf16),
            jax.ShapeDtypeStruct((2, 1024, WIDE), bf16),
            jax.ShapeDtypeStruct((STEPS, BS, BS), f32),
            jax.ShapeDtypeStruct((8, WIDE), f32),
            jax.ShapeDtypeStruct((8, 8, BS), f32),
        ),
        in_specs=[SM, SM, VM, VM, VM],
        out_specs=(VM,) * 5,
        scratch_shapes=[
            vmem((NQ, BS, BS), f32),
            vmem((STEPS, BS, WIDE), f32),
            vmem((WIDE, WIDE), f32),
            vmem((BS, BS), f32),
            vmem((BS, BS), f32),
            vmem((BS, BS), f32),
            vmem((2, 2, 8, 2, BS, BS), f32),
            vmem((WIDE, WIDE), bf16),
            vmem((WIDE, WIDE), bf16),
            vmem((8, CHUNKS[0][1], 8, BS), f32),
            vmem((8, CHUNKS[1][1], 8, BS), f32),
            vmem((NQ, 8, BS), f32),
            vmem((8, CHUNKS[0][1], 8, BS), f32),
            vmem((8, CHUNKS[1][1], 8, BS), f32),
            vmem((8, 2, BS, BS), f32),
            vmem((2, BS, BS), f32),
            vmem((8, 8, BS), f32),
            vmem((8, BS), f32),
            vmem((8, 8, BS), f32),
            vmem((8, BS), f32),
            vmem((8, BS), f32),
        ]
        + [sem((2, 8))] * 8
        + [sem((8,))] * 6
        + [sem((2, 8))] * 2
        + [sem((8,))] * 6
        + [sem, sem],
        compiler_params=pltpu.CompilerParams(
            collective_id=0, has_side_effects=True, vmem_limit_bytes=40 << 20
        ),
        name="exchange",
    )(mem, pat, scand, ccand, pg)


def update_kernel(mem, pat, diag, x_hi, x_lo, y, g, hess, out, grad_out, rows, in_sem, out_sem):
    r = lax.axis_index("prow")
    c = lax.axis_index("pcol")

    def load(a):
        return pltpu.make_async_copy(hess.at[a], rows.at[a], in_sem.at[a])

    def save(a):
        return pltpu.make_async_copy(rows.at[a], out.at[a], out_sem.at[a])

    for a in range(8):
        load(a).start()

    def is_pivot(i):
        pivot = i == member(mem, 0)
        for k in range(1, STEPS):
            pivot = jnp.logical_or(pivot, i == member(mem, k))
        return pivot

    dec = dot3(split(jnp.concatenate([y[...], y[...]], axis=0)), (x_hi[0], x_lo[0]))
    for a in range(8):
        i = 8 * a + r
        val = g[a, pl.ds(r, 1), :] - dec[0:1, BS * a : BS * a + BS]
        for k in range(STEPS):
            val = jnp.where(i == member(mem, k), y[0:1, BS * k : BS * k + BS], val)
        grad_out[a : a + 1, :] = val

    rr = lax.broadcasted_iota(jnp.int32, (BS, BS), 0)
    cc = lax.broadcasted_iota(jnp.int32, (BS, BS), 1)
    shift = jnp.where(rr == cc, SHIFT, 0.0)
    cols = (x_hi[1], x_lo[1])

    def two_rows(t):
        at = pl.ds(pl.multiple_of(2 * BS * t, 2 * BS), 2 * BS)
        upd = dot3((x_hi[0, at, :], x_lo[0, at, :]), cols)
        for e in range(2):
            a = 2 * t + e
            i = 8 * a + r
            live = jnp.where(is_pivot(i), 0.0, 1.0).astype(f32)
            load(a).wait()
            for b in range(8):
                j = 8 * b + c
                keep = live * pat[i, j].astype(f32)
                on = jnp.where(i == j, 1.0, 0.0).astype(f32) * live
                sub = upd[BS * e : BS * e + BS, BS * b : BS * b + BS]
                there = pl.ds(b, BS, stride=8)
                rows[a, there, :] = keep * (rows[a, there, :] - sub) + on * shift
            for k in range(STEPS):
                pk = member(mem, k)

                @pl.when(lax.rem(pk, 8) == c)
                def _():
                    there = pl.ds(pk // 8, BS, stride=8)
                    mine = pl.ds(pl.multiple_of(BS * a, BS), BS)
                    part = slice(BS * k, BS * k + BS)

                    @pl.when(i != pk)
                    def _():
                        rows[a, there, :] = x_hi[0, mine, part].astype(f32) + x_lo[0, mine, part].astype(f32)

                    @pl.when(i == pk)
                    def _():
                        rows[a, there, :] = diag[k]
            save(a).start()

    loop(0, 4, two_rows)
    for a in range(8):
        save(a).wait()


def update(mem, pat, diag, x_hi, x_lo, y, g, hess):
    return pl.pallas_call(
        update_kernel,
        out_shape=(
            jax.ShapeDtypeStruct(hess.shape, f32),
            jax.ShapeDtypeStruct((8, BS), f32),
        ),
        in_specs=[SM, SM, VM, VM, VM, VM, VM, ANY],
        out_specs=(ANY, VM),
        scratch_shapes=[
            pltpu.VMEM((8, 1024, BS), f32),
            pltpu.SemaphoreType.DMA((8,)),
            pltpu.SemaphoreType.DMA((8,)),
        ],
        compiler_params=pltpu.CompilerParams(vmem_limit_bytes=32 << 20),
        name="update",
    )(mem, pat, diag, x_hi, x_lo, y, g, hess)


def shards(
    poses, codebook, offsets, confidence, code_ids, creature_ids, hess_raw, pattern, membership
):
    scand, ccand, pg = prepare(
        membership, hess_raw.reshape(8, BS, 8, 1, BS), poses, codebook, offsets,
        confidence.reshape(16, BS), code_ids.reshape(16, BS), creature_ids.reshape(16, BS),
    )
    x_hi, x_lo, diag, y, g = exchange(membership, pattern, scand, ccand, pg.reshape(8, 8, BS))
    state, grad = update(
        membership, pattern, diag, x_hi, x_lo, y, g, hess_raw.reshape(8, 1024, BS)
    )
    return state.reshape(hess_raw.shape), grad.reshape(8, 1, BS)


def solution(mesh):
    return jax.shard_map(
        shards,
        mesh=mesh,
        in_specs=(
            P(("frames", "prow", "pcol"), None),
            P(),
            P(),
            P(("frames", "prow", "pcol")),
            P(("frames", "prow", "pcol")),
            P(("frames", "prow", "pcol")),
            P(None, "prow", None, None, "pcol", None),
            P(),
            P(),
        ),
        out_specs=(P(None, "prow", None, None, "pcol", None), P(None, "prow", None)),
        check_vma=False,
    )
```

time: 1800 us -> 120 us (0.07)
  the two profiles are of different devices: /device:TPU:105 before, /device:TPU:11 now
where the time goes in v2:
time: 120 us
  Pallas kernels  112 us (93%)
  local copies, waits for them, and re-layouts  7.62 us (6%)
    pallas_call x1, Pallas kernels, exchange(): pl.pallas_call(exchange_kernel, out_shape=(jax.ShapeDtypeStruct((2, 1024,...  99.5 us
    pallas_call x1, Pallas kernels, update(): pl.pallas_call(update_kernel, out_shape=(jax.ShapeDtypeStruct(hess.shape,...  9.65 us
    unnamed x22, local copies, waits for them, and re-layouts  7.62 us
    pallas_call x1, Pallas kernels, prepare(): pl.pallas_call(prepare_kernel, out_shape=(jax.ShapeDtypeStruct((NQ, BS, B...  2.57 us

profile of v2, /device:TPU:11, one launch (start us, length us, event | category | flops | bytes accessed | tf_op | source)
XLA Modules:
  0.0 120.0 jit_solution(12241617123077323855)
XLA Ops:
  0.6 0.0 copy-start.7
  0.6 0.0 copy-start
  0.7 2.2 %copy-done = f32[8,1,128,8,1,128]{5,4,3,2,1,0:T(1,128)S(1)} copy-done((f32[8,1,128,8,1,128]{5,4,3,2,1,0:T(1,128)S(1)}, f32[8,1,128,8,1,128]{5,4,3,2,1,0:T(1,128)}, u32[]{:S(2)}) %copy-start) | copy-done | bytes 4194328
  2.8 0.0 copy-start.2
  2.8 1.2 %copy-done.2 = bf16[2048,256]{1,0:T(8,128)(2,1)S(1)} copy-done((bf16[2048,256]{1,0:T(8,128)(2,1)S(1)}, bf16[2048,256]{1,0:T(8,128)(2,1)}, u32[]{:S(2)}) %copy-start.2) | copy-done | bytes 1048600
  4.1 0.0 copy-start.4
  4.1 0.7 copy-done.4
  4.8 0.0 copy-start.5
  4.8 0.7 copy-done.5
  5.5 0.0 copy-start.6
  5.5 0.7 copy-done.6
  6.2 0.0 copy-start.8
  6.2 0.7 copy-done.8
  6.9 0.0 copy-start.9
  6.9 0.7 copy-done.9
  7.6 0.0 copy-start.10
  7.6 0.7 copy-done.10
  8.3 0.0 copy-start.3
  8.3 0.0 copy-start.1
  8.3 2.6 %prepare.1 = (f32[10,128,128]{2,1,0:T(8,128)S(1)}, f32[8,2,128,128]{3,2,1,0:T(8,128)S(1)}, f32[64,128]{1,0:T(8,128)S(1)}) custom-call(s32[2,2]{1,0:T(2,128)S(1)} %copy-done.6, f32[8,128,8,1,128]{4,3,2,1,0:T(1,128)S(1)} %bitcast.12, bf16[2048,256]{1,0:T(8,128)(2,1)S(1)} %copy-done.2, bf16[32,256]{1,0:T(8,128)(2,1)S(1)} %copy-done.4, ...), custom_call_target="tpu_custom_call" | custom-call | tf_op jit(solution)/shard_map/prepare/pallas_call | solution.py:127
  10.8 0.0 copy-done.7
  10.9 0.0 copy-done.3
  10.9 99.5 %exchange.1 = (bf16[2,1024,512]{2,1,0:T(8,128)(2,1)S(1)}, bf16[2,1024,512]{2,1,0:T(8,128)(2,1)S(1)}, f32[4,128,128]{2,1,0:T(8,128)S(1)}, f32[8,512]{1,0:T(8,128)S(1)}, f32[8,8,128]{2,1,0:T(8,128)S(1)}) custom-call(s32[2,2]{1,0:T(2,128)S(1)} %copy-done.7, s32[64,64]{1,0:T(8,128)S(1)} %copy-done.3, f32[10,128,128]{2,1,0:T(8,128)S(1)} %get-tuple-element.12.scand, ...), custom_call_target="tpu_custom_call" | custom-call | tf_op jit(solution)/shard_map/exchange/pallas_call | solution.py:528
  110.3 0.0 copy-done.1
  110.3 9.6 %update.1 = (f32[8,1024,128]{2,1,0:T(8,128)}, f32[8,128]{1,0:T(8,128)}) custom-call(s32[2,2]{1,0:T(2,128)S(1)} %copy-done.7, s32[64,64]{1,0:T(8,128)S(1)} %copy-done.3, f32[4,128,128]{2,1,0:T(8,128)S(1)} %get-tuple-element.15.diag, bf16[2,1024,512]{2,1,0:T(8,128)(2,1)S(1)} %get-tuple-element.16.x_hi, bf16[2,1024,512]{2,1,0:T(8,128)(2,1)S(1)} %get-tuple-element.17.x_lo, ...), custom_call_target="tpu_custom_call" | custom-call | tf_op jit(solution)/shard_map/update/pallas_call | solution.py:645
Async XLA Ops:
  0.6 10.2 %copy-start.7 = (s32[2,2]{1,0:T(2,128)S(1)}, s32[2,2]{1,0:T(2,128)}, u32[]{:S(2)}) copy-start(s32[2,2]{1,0:T(2,128)} %mem.5) | copy-start | bytes 52
  0.6 2.2 %copy-start = (f32[8,1,128,8,1,128]{5,4,3,2,1,0:T(1,128)S(1)}, f32[8,1,128,8,1,128]{5,4,3,2,1,0:T(1,128)}, u32[]{:S(2)}) copy-start(f32[8,1,128,8,1,128]{5,4,3,2,1,0:T(1,128)} %param.15) | copy-start | bytes 12582916
  2.8 1.2 %copy-start.2 = (bf16[2048,256]{1,0:T(8,128)(2,1)S(1)}, bf16[2048,256]{1,0:T(8,128)(2,1)}, u32[]{:S(2)}) copy-start(bf16[2048,256]{1,0:T(8,128)(2,1)} %poses.1) | copy-start | bytes 3145732
  4.1 0.7 copy-start.4
  4.8 0.7 copy-start.5
  5.5 0.7 copy-start.6
  6.2 0.7 copy-start.8
  6.9 0.7 copy-start.9
  7.6 0.7 copy-start.10
  8.3 2.6 %copy-start.3 = (s32[64,64]{1,0:T(8,128)S(1)}, s32[64,64]{1,0:T(8,128)}, u32[]{:S(2)}) copy-start(s32[64,64]{1,0:T(8,128)} %pat.3) | copy-start | bytes 49156
  8.3 102.1 %copy-start.1 = (f32[8,1,128,8,1,128]{5,4,3,2,1,0:T(1,128)S(1)}, f32[8,1,128,8,1,128]{5,4,3,2,1,0:T(1,128)}, u32[]{:S(2)}) copy-start(f32[8,1,128,8,1,128]{5,4,3,2,1,0:T(1,128)} %param.15) | copy-start | bytes 12582916

commit v3 on v2

--- a/solution.py
+++ b/solution.py
@@ -53,7 +53,21 @@
 ANY = pl.BlockSpec(memory_space=pl.ANY)
 
 
-def prepare_kernel(mem, hess, poses, codebook, offsets, conf, codes, kinds, scand, ccand, pg, sem):
+def prepare_kernel(
+    mem, hess, poses_at, codebook_at, offsets_at, conf_at, codes_at, kinds_at, scand, ccand, pg,
+    poses, codebook, offsets, conf, codes, kinds, sem, in_sem,
+):
+    fetches = [
+        pltpu.make_async_copy(src, dst, in_sem.at[n])
+        for n, (src, dst) in enumerate(
+            [
+                (codes_at, codes), (conf_at, conf), (kinds_at, kinds),
+                (poses_at, poses), (codebook_at, codebook), (offsets_at, offsets),
+            ]
+        )
+    ]
+    for fetch in fetches:
+        fetch.start()
     f = lax.axis_index("frames")
     slot = [member(mem, k) // 8 for k in range(STEPS)]
     copies = [
@@ -82,6 +96,8 @@
         for copy in by_row:
             copy.start()
 
+    for fetch in fetches:
+        fetch.wait()
     ids = lax.broadcasted_iota(jnp.int32, (CODES, BS), 0)
     weights, marks = [], []
     for s in range(16):
@@ -131,9 +147,10 @@
             jax.ShapeDtypeStruct((8, 2, BS, BS), f32),
             jax.ShapeDtypeStruct((64, BS), f32),
         ),
-        in_specs=[SM, ANY, VM, VM, VM, VM, VM, VM],
+        in_specs=[SM] + [ANY] * 7,
         out_specs=(VM, VM, VM),
-        scratch_shapes=[pltpu.SemaphoreType.DMA((NQ + 18,))],
+        scratch_shapes=[pltpu.VMEM(x.shape, x.dtype) for x in (poses, codebook, offsets, conf, codes, kinds)]
+        + [pltpu.SemaphoreType.DMA((NQ + 18,)), pltpu.SemaphoreType.DMA((6,))],
         compiler_params=pltpu.CompilerParams(vmem_limit_bytes=24 << 20),
         name="prepare",
     )(mem, hess, poses, codebook, offsets, conf, codes, kinds)
@@ -199,10 +216,10 @@
     mem, pat, scand, ccand, pg,
     x_hi, x_lo, diag, y_out, g_out,
     s_all, low, inv, cur, fac_u, fac_i, raw, wh, wl,
-    s1r_a, s1r_b, s1, s2r_a, s2r_b, par, mine, g1r, g1, g2r, g2, g3r,
+    s1r_a, s1r_b, s1, s2r_a, s2r_b, par, picked, other, both, mine, g1r, g1, g2r, g2, g3r,
     snd_s1, rcv_s1, snd_s2, rcv_s2, snd_s3, rcv_s3, snd_sx, rcv_sx,
-    snd_a, rcv_a, snd_r, rcv_r, snd_t, rcv_t, snd_x, rcv_x,
-    snd_g1, rcv_g1, snd_g2, rcv_g2, snd_g4, rcv_g4, snd_g3, rcv_g3,
+    snd_x, rcv_x, snd_a, rcv_a, snd_r2, snd_t2, snd_t1, rcv_r, rcv_t,
+    snd_g1, rcv_g1, snd_g2, rcv_g2, snd_g4, rcv_g4, snd_g3, rcv_g3, snd_b, rcv_b, snd_r1,
 ):
     s1r, s2r = (s1r_a, s1r_b), (s2r_a, s2r_b)
     f = lax.axis_index("frames")
@@ -216,6 +233,27 @@
 
     sibling = (1 - f, r, c)
 
+    def q_at(line, pair):
+        return 2 * line + pair + f * (3 * pair - line)
+
+    def p_at(line, pair):
+        return line + 4 * pair + f * (line - 3 * pair)
+
+    def q_parts(v):
+        return v // 2 + f * (lax.rem(v, 4) - v // 2), lax.rem(v, 2) + f * (v // 4 - lax.rem(v, 2))
+
+    def p_parts(v):
+        return lax.rem(v, 4) + f * (v // 2 - lax.rem(v, 4)), v // 4 + f * (lax.rem(v, 2) - v // 4)
+
+    ql, qh = q_parts(q)
+    pl_, ph = p_parts(p)
+
+    def q_line(d):
+        return lax.rem(ql + d, 4)
+
+    def p_line(d):
+        return lax.rem(pl_ + d, 4)
+
     def copy(src, dst, snd, rcv, to):
         return pltpu.make_async_remote_copy(
             src_ref=src, dst_ref=dst, send_sem=snd, recv_sem=rcv, device_id=to, device_id_type=MESH
@@ -246,18 +284,21 @@
 
     loop(1, 8, greet_line)
 
-    def greet_turn(d):
-        @pl.when(jnp.logical_or(d != p, p != q))
+    def at_home(p_to, q_to):
+        return jnp.logical_and(p_to == p, q_to == q)
+
+    def away(p_to, q_to, fn):
+        @pl.when(jnp.logical_not(at_home(p_to, q_to)))
         def _():
-            greet(place(d, p))
-
-        @pl.when(jnp.logical_or(d != q, p != q))
-        def _():
-            greet(place(q, d))
-
-    loop(0, 8, greet_turn)
-    same = jnp.where(p == q, 1, 0)
-    pl.semaphore_wait(barrier, 31 - 2 * same)
+            fn()
+
+    def greet_turn(e):
+        away(p_at(ql, e), p, lambda: greet(place(p_at(ql, e), p)))
+        away(q, q_at(pl_, e), lambda: greet(place(q, q_at(pl_, e))))
+
+    loop(0, 2, greet_turn)
+    same = jnp.where(jnp.logical_and(p == q, ql == pl_), 1, 0)
+    pl.semaphore_wait(barrier, 19 - 2 * same)
 
     def rows_of(slice_id):
         return pl.ds(pl.multiple_of(8 * slice_id, 8), 8)
@@ -295,14 +336,27 @@
     def g4_copy(peer, at):
         return copy(g_out.at[at], g_out.at[at], snd_g4.at[peer], rcv_g4.at[at], (f, r, peer))
 
-    def a_copy(peer, at):
-        return copy(ccand.at[peer], par.at[at], snd_a.at[peer], rcv_a.at[at], place(p, peer))
-
-    def r_copy(peer, at):
-        return copy(mine, raw.at[f, f, at], snd_r.at[peer], rcv_r.at[at], place(p, peer))
-
-    def t_copy(peer, at):
-        return copy(mine, raw.at[1 - f, f, at], snd_t.at[peer], rcv_t.at[at], place(peer, p))
+    def a_copy(e, line, at):
+        return copy(
+            ccand.at[q_at(line, e)], par.at[at, e], snd_a.at[e, line], rcv_a.at[e, at], place(p, q_at(line, qh))
+        )
+
+    def b_copy():
+        return copy(picked.at[1 - qh], other, snd_b, rcv_b, place(p, q_at(ql, 1 - qh)))
+
+    def r1_copy(at):
+        return copy(mine, raw.at[f, f, at], snd_r1, rcv_r.at[at], place(p, q_at(ql, 1 - qh)))
+
+    def r2_copy(e, line, at):
+        part = raw.at[f, f, at]
+        return copy(part, part, snd_r2.at[e, line], rcv_r.at[at], place(p, q_at(line, qh)))
+
+    def t1_copy(e, at):
+        return copy(mine, raw.at[1 - f, f, at], snd_t1.at[e], rcv_t.at[at], place(p_at(ql, e), p))
+
+    def t2_copy(e, line, at):
+        part = raw.at[1 - f, f, at]
+        return copy(part, part, snd_t2.at[e, line], rcv_t.at[at], place(p_at(line, ph), q))
 
     def x_copy(which, at, core):
         part = raw.at[which, core, at]
@@ -314,7 +368,8 @@
     for h, (lo, n) in enumerate(CHUNKS):
         s1r[h][q] = scand[lo : lo + n, rows_of(q + 8 * f), :]
     g1r[c] = pg[c]
-    par[q] = ccand[q]
+    for e in range(2):
+        par[ql, e] = ccand[q_at(ql, e)]
 
     for h in range(2):
         lo, n = CHUNKS[h]
@@ -331,6 +386,8 @@
     loop(1, 8, lambda d: g2_copy(r_peer(d), r).start())
     g2r[r] = g1[...]
 
+    for e in range(2):
+        loop(1, 4, lambda d: a_copy(e, q_line(d), ql).start())
 
     for h in range(2):
         lo, n = CHUNKS[h]
@@ -342,7 +399,6 @@
         loop(1, 8, lambda d: s3_copy(h, q_peer(d), q).start())
         sx_copy(h, q, f).start()
 
-    loop(1, 8, lambda d: a_copy(q_peer(d), q).start())
 
     loop(1, 8, lambda d: g2_copy(r_peer(d), r_peer(d)).wait())
     g2[...] = jnp.sum(g2r[...], axis=0)
@@ -358,8 +414,6 @@
 
     def sx_ready(h):
         loop(0, 8, lambda at: sx_copy(h, at, 1 - f).wait_recv())
-
-    pass_on(0)
 
     rr = lax.broadcasted_iota(jnp.int32, (BS, BS), 0)
     cc = lax.broadcasted_iota(jnp.int32, (BS, BS), 1)
@@ -394,41 +448,59 @@
         diag[k] = lower
         if k == 0:
             pass_on(1)
-        if k == 1:
-            spread_panels()
+            spread_on()
         if k == 2:
             g3.wait()
             g_out[c] = g2[...] + g3r[...]
             loop(1, 8, lambda d: g4_copy(c_peer(d), c).start())
 
-    def spread_panels():
-        loop(1, 8, lambda d: a_copy(q_peer(d), q_peer(d)).wait())
+    def owner(k):
+        return q_parts(lax.rem(mem[f, k], 8))
+
+    def pick():
+        for e in range(2):
+            loop(1, 4, lambda d: a_copy(e, q_line(d), q_line(d)).wait())
+        for e in range(2):
+            for k in range(2):
+                picked[e, k] = par[owner(k)[0], e, k]
+        b_copy().start()
+
+    def spread_mine():
+        b_copy().wait()
+        both[qh] = picked[qh]
+        both[1 - qh] = other[...]
 
         @pl.when(f == 0)
         def _():
             for k in range(2):
-                mine[k] = par[lax.rem(mem[0, k], 8), k]
+                mine[k] = both[lax.rem(mem[0, k], 2), k]
 
         @pl.when(f == 1)
         def _():
             for k in range(2):
-                mine[k] = par[lax.rem(mem[1, k], 8), k].T
-
-        loop(1, 8, lambda d: r_copy(q_peer(d), q).start())
+                mine[k] = both[lax.rem(mem[1, k], 8) // 4, k].T
+
+        r1_copy(q).start()
+        for e in range(2):
+            away(p_at(ql, e), p, lambda: t1_copy(e, q).start())
         raw[f, f, q] = mine[...]
 
-        def turn(d):
-            @pl.when(jnp.logical_or(d != p, p != q))
-            def _():
-                t_copy(d, q).start()
-
-        loop(0, 8, turn)
-
-        @pl.when(p == q)
+        @pl.when(jnp.logical_and(p == q, ql == pl_))
         def _():
             raw[1 - f, f, q] = mine[...]
 
         x_copy(f, q, f).start()
+
+    def spread_on():
+        r1_copy(q_at(ql, 1 - qh)).wait_recv()
+        for e in range(2):
+            loop(1, 4, lambda d: r2_copy(e, q_line(d), q_at(ql, e)).start())
+        for e in range(2):
+            at = q_at(pl_, e)
+            away(q, at, lambda: t1_copy(e, at).wait_recv())
+            loop(1, 4, lambda d: t2_copy(e, p_line(d), at).start())
+            x_copy(1 - f, at, f).start()
+        x_copy(f, q_at(ql, 1 - qh), f).start()
 
     def step(k):
         for kk in range(STEPS):
@@ -444,22 +516,21 @@
             def _():
                 after(kk)
 
+    pick()
+    pass_on(0)
+    spread_mine()
     loop(0, STEPS, step)
 
-    def r_arrives(d):
-        r_copy(q_peer(d), q_peer(d)).wait_recv()
-        x_copy(f, q_peer(d), f).start()
-
-    loop(1, 8, r_arrives)
-
-    def t_arrives(b):
-        @pl.when(jnp.logical_or(b != q, p != q))
-        def _():
-            t_copy(b, b).wait_recv()
-
-        x_copy(1 - f, b, f).start()
-
-    loop(0, 8, t_arrives)
+    def arrives(d):
+        for e in range(2):
+            at = q_at(q_line(d), e)
+            r2_copy(e, q_line(d), at).wait_recv()
+            x_copy(f, at, f).start()
+            at = q_at(p_line(d), e)
+            t2_copy(e, p_line(d), at).wait_recv()
+            x_copy(1 - f, at, f).start()
+
+    loop(1, 4, arrives)
 
     h, l = split(inv[...])
     wh[...] = h
@@ -476,50 +547,62 @@
     gp = jnp.broadcast_to(gp, (16, WIDE))
     y_out[...] = dot3(split(gp), (wh[...], wl[...]))[0:8]
 
-    def panel(which, a):
+    def panel(which, t):
         base = r + which * (c - r)
-        i = 8 * a + base
-        pivot = i == member(mem, 0)
-        for k in range(1, STEPS):
-            pivot = jnp.logical_or(pivot, i == member(mem, k))
-        z = jnp.where(pivot, 0.0, 1.0).astype(f32)
-        m1 = z * pat[i, member(mem, 0)].astype(f32)
-        m2 = z * pat[i, member(mem, 2)].astype(f32)
-        one = split(jnp.concatenate([raw[which, 0, a, 0], raw[which, 0, a, 1]], axis=1) * m1)
-        two = split(jnp.concatenate([raw[which, 1, a, 0], raw[which, 1, a, 1]], axis=1))
-        rows = pl.ds(pl.multiple_of(BS * a, BS), BS)
-        for lo, x in ((0, dot3(one, w11)), (half, m2 * (dot3(one, w21) + dot3(two, w22)))):
-            hi, rest = split(x)
-            x_hi[which, rows, lo : lo + half] = hi
-            x_lo[which, rows, lo : lo + half] = rest
-
-    def panel_step(t):
-        which = t // 8
-        a = lax.rem(t, 8)
-        x_copy(which, a, 1 - f).wait_recv()
-        panel(which, a)
-
-    loop(0, 16, panel_step)
+        ones, twos, keeps = [], [], []
+        for e in range(2):
+            a = 2 * t + e
+            x_copy(which, a, 1 - f).wait_recv()
+        for e in range(2):
+            a = 2 * t + e
+            i = 8 * a + base
+            pivot = i == member(mem, 0)
+            for k in range(1, STEPS):
+                pivot = jnp.logical_or(pivot, i == member(mem, k))
+            z = jnp.where(pivot, 0.0, 1.0).astype(f32)
+            m1 = z * pat[i, member(mem, 0)].astype(f32)
+            m2 = z * pat[i, member(mem, 2)].astype(f32)
+            ones.append(jnp.concatenate([raw[which, 0, a, 0], raw[which, 0, a, 1]], axis=1) * m1)
+            twos.append(jnp.concatenate([raw[which, 1, a, 0], raw[which, 1, a, 1]], axis=1))
+            keeps.append(m2)
+        one = split(jnp.concatenate(ones, axis=0))
+        two = split(jnp.concatenate(twos, axis=0))
+        second = dot3(one, w21) + dot3(two, w22)
+        rows = pl.ds(pl.multiple_of(half * t, half), half)
+        hi, rest = split(dot3(one, w11))
+        x_hi[which, rows, 0:half] = hi
+        x_lo[which, rows, 0:half] = rest
+        second = jnp.concatenate([second[0:BS] * keeps[0], second[BS:half] * keeps[1]], axis=0)
+        hi, rest = split(second)
+        x_hi[which, rows, half:WIDE] = hi
+        x_lo[which, rows, half:WIDE] = rest
+
+    loop(0, 8, lambda t: panel(t // 4, lax.rem(t, 4)))
 
     def tail(d):
         for h in range(2):
             s3_copy(h, q_peer(d), q).wait_send()
-        r_copy(q_peer(d), q).wait_send()
         g4_copy(c_peer(d), c).wait_send()
 
     loop(1, 8, tail)
-
-    def tail_turn(d):
-        @pl.when(jnp.logical_or(d != p, p != q))
-        def _():
-            t_copy(d, q).wait_send()
-
+    r1_copy(q).wait_send()
+    for e in range(2):
+        away(p_at(ql, e), p, lambda: t1_copy(e, q).wait_send())
+
+    def tail_line(d):
+        for e in range(2):
+            r2_copy(e, q_line(d), q_at(ql, e)).wait_send()
+            t2_copy(e, p_line(d), q_at(pl_, e)).wait_send()
+
+    loop(1, 4, tail_line)
+
+    def tail_pair(d):
         for h in range(2):
             sx_copy(h, d, f).wait_send()
         for which in range(2):
             x_copy(which, d, f).wait_send()
 
-    loop(0, 8, tail_turn)
+    loop(0, 8, tail_pair)
 
 
 def exchange(mem, pat, scand, ccand, pg):
@@ -551,7 +634,10 @@
             vmem((NQ, 8, BS), f32),
             vmem((8, CHUNKS[0][1], 8, BS), f32),
             vmem((8, CHUNKS[1][1], 8, BS), f32),
-            vmem((8, 2, BS, BS), f32),
+            vmem((4, 2, 2, BS, BS), f32),
+            vmem((2, 2, BS, BS), f32),
+            vmem((2, BS, BS), f32),
+            vmem((2, 2, BS, BS), f32),
             vmem((2, BS, BS), f32),
             vmem((8, 8, BS), f32),
             vmem((8, BS), f32),
@@ -559,11 +645,11 @@
             vmem((8, BS), f32),
             vmem((8, BS), f32),
         ]
-        + [sem((2, 8))] * 8
-        + [sem((8,))] * 6
-        + [sem((2, 8))] * 2
-        + [sem((8,))] * 6
-        + [sem, sem],
+        + [sem((2, 8))] * 10
+        + [sem((2, 4))] * 4
+        + [sem((2,))]
+        + [sem((8,))] * 8
+        + [sem] * 5,
         compiler_params=pltpu.CompilerParams(
             collective_id=0, has_side_effects=True, vmem_limit_bytes=40 << 20
         ),

time: 120 us -> 98.7 us (0.82)
  the two profiles are of different devices: /device:TPU:11 before, /device:TPU:105 now
where the time goes in v3:
time: 98.7 us; the launch traced here: 98.3 us
  Pallas kernels  89.8 us (91%)
  local copies, waits for them, and re-layouts  7.62 us (8%)
    pallas_call x1, Pallas kernels, exchange(): pl.pallas_call(exchange_kernel, out_shape=(jax.ShapeDtypeStruct((2, 1024,...  77.4 us
    pallas_call x1, Pallas kernels, update(): pl.pallas_call(update_kernel, out_shape=(jax.ShapeDtypeStruct(hess.shape,...  9.65 us
    unnamed x22, local copies, waits for them, and re-layouts  7.62 us
    pallas_call x1, Pallas kernels, prepare(): pl.pallas_call(prepare_kernel, out_shape=(jax.ShapeDtypeStruct((NQ, BS, B...  2.77 us

profile of v3, /device:TPU:105, one launch (start us, length us, event | category | flops | bytes accessed | tf_op | source)
XLA Modules:
  0.0 98.3 jit_solution(13828286946539174268)
XLA Ops:
  0.6 0.0 copy-start.7
  0.6 0.0 copy-start
  0.7 2.2 %copy-done = f32[8,1,128,8,1,128]{5,4,3,2,1,0:T(1,128)S(1)} copy-done((f32[8,1,128,8,1,128]{5,4,3,2,1,0:T(1,128)S(1)}, f32[8,1,128,8,1,128]{5,4,3,2,1,0:T(1,128)}, u32[]{:S(2)}) %copy-start) | copy-done | bytes 4194328
  2.8 0.0 copy-start.2
  2.8 1.2 %copy-done.2 = bf16[2048,256]{1,0:T(8,128)(2,1)S(1)} copy-done((bf16[2048,256]{1,0:T(8,128)(2,1)S(1)}, bf16[2048,256]{1,0:T(8,128)(2,1)}, u32[]{:S(2)}) %copy-start.2) | copy-done | bytes 1048600
  4.1 0.0 copy-start.4
  4.1 0.7 copy-done.4
  4.8 0.0 copy-start.5
  4.8 0.7 copy-done.5
  5.5 0.0 copy-start.6
  5.5 0.7 copy-done.6
  6.2 0.0 copy-start.8
  6.2 0.7 copy-done.8
  6.9 0.0 copy-start.9
  6.9 0.7 copy-done.9
  7.6 0.0 copy-start.10
  7.6 0.7 copy-done.10
  8.3 0.0 copy-start.3
  8.3 0.0 copy-start.1
  8.3 2.8 %prepare.1 = (f32[10,128,128]{2,1,0:T(8,128)S(1)}, f32[8,2,128,128]{3,2,1,0:T(8,128)S(1)}, f32[64,128]{1,0:T(8,128)S(1)}) custom-call(s32[2,2]{1,0:T(2,128)S(1)} %copy-done.6, f32[8,128,8,1,128]{4,3,2,1,0:T(1,128)S(1)} %bitcast.12, bf16[2048,256]{1,0:T(8,128)(2,1)S(1)} %copy-done.2, bf16[32,256]{1,0:T(8,128)(2,1)S(1)} %copy-done.4, ...), custom_call_target="tpu_custom_call" | custom-call | tf_op jit(solution)/shard_map/prepare/pallas_call | solution.py:143
  11.1 0.0 copy-done.7
  11.1 0.0 copy-done.3
  11.1 77.4 %exchange.1 = (bf16[2,1024,512]{2,1,0:T(8,128)(2,1)S(1)}, bf16[2,1024,512]{2,1,0:T(8,128)(2,1)S(1)}, f32[4,128,128]{2,1,0:T(8,128)S(1)}, f32[8,512]{1,0:T(8,128)S(1)}, f32[8,8,128]{2,1,0:T(8,128)S(1)}) custom-call(s32[2,2]{1,0:T(2,128)S(1)} %copy-done.7, s32[64,64]{1,0:T(8,128)S(1)} %copy-done.3, f32[10,128,128]{2,1,0:T(8,128)S(1)} %get-tuple-element.12.scand, ...), custom_call_target="tpu_custom_call" | custom-call | tf_op jit(solution)/shard_map/exchange/pallas_call | solution.py:611
  88.5 0.0 copy-done.1
  88.5 9.6 %update.1 = (f32[8,1024,128]{2,1,0:T(8,128)}, f32[8,128]{1,0:T(8,128)}) custom-call(s32[2,2]{1,0:T(2,128)S(1)} %copy-done.7, s32[64,64]{1,0:T(8,128)S(1)} %copy-done.3, f32[4,128,128]{2,1,0:T(8,128)S(1)} %get-tuple-element.15.diag, bf16[2,1024,512]{2,1,0:T(8,128)(2,1)S(1)} %get-tuple-element.16.x_hi, bf16[2,1024,512]{2,1,0:T(8,128)(2,1)S(1)} %get-tuple-element.17.x_lo, ...), custom_call_target="tpu_custom_call" | custom-call | tf_op jit(solution)/shard_map/update/pallas_call | solution.py:731
Async XLA Ops:
  0.6 10.4 %copy-start.7 = (s32[2,2]{1,0:T(2,128)S(1)}, s32[2,2]{1,0:T(2,128)}, u32[]{:S(2)}) copy-start(s32[2,2]{1,0:T(2,128)} %mem.5) | copy-start | bytes 52
  0.6 2.2 %copy-start = (f32[8,1,128,8,1,128]{5,4,3,2,1,0:T(1,128)S(1)}, f32[8,1,128,8,1,128]{5,4,3,2,1,0:T(1,128)}, u32[]{:S(2)}) copy-start(f32[8,1,128,8,1,128]{5,4,3,2,1,0:T(1,128)} %param.15) | copy-start | bytes 12582916
  2.8 1.2 %copy-start.2 = (bf16[2048,256]{1,0:T(8,128)(2,1)S(1)}, bf16[2048,256]{1,0:T(8,128)(2,1)}, u32[]{:S(2)}) copy-start(bf16[2048,256]{1,0:T(8,128)(2,1)} %poses_at.1) | copy-start | bytes 3145732
  4.1 0.7 copy-start.4
  4.8 0.7 copy-start.5
  5.5 0.7 copy-start.6
  6.2 0.7 copy-start.8
  6.9 0.7 copy-start.9
  7.6 0.7 copy-start.10
  8.3 2.8 %copy-start.3 = (s32[64,64]{1,0:T(8,128)S(1)}, s32[64,64]{1,0:T(8,128)}, u32[]{:S(2)}) copy-start(s32[64,64]{1,0:T(8,128)} %pat.3) | copy-start | bytes 49156
  8.3 80.2 %copy-start.1 = (f32[8,1,128,8,1,128]{5,4,3,2,1,0:T(1,128)S(1)}, f32[8,1,128,8,1,128]{5,4,3,2,1,0:T(1,128)}, u32[]{:S(2)}) copy-start(f32[8,1,128,8,1,128]{5,4,3,2,1,0:T(1,128)} %param.15) | copy-start | bytes 12582916

commit v4 on v3

--- a/solution.py
+++ b/solution.py
@@ -51,6 +51,7 @@
 VM = pl.BlockSpec(memory_space=pltpu.VMEM)
 SM = pl.BlockSpec(memory_space=pltpu.SMEM)
 ANY = pl.BlockSpec(memory_space=pl.ANY)
+HBM = pl.BlockSpec(memory_space=pltpu.HBM)
 
 
 def prepare_kernel(
@@ -147,7 +148,7 @@
             jax.ShapeDtypeStruct((8, 2, BS, BS), f32),
             jax.ShapeDtypeStruct((64, BS), f32),
         ),
-        in_specs=[SM] + [ANY] * 7,
+        in_specs=[SM] + [HBM] * 7,
         out_specs=(VM, VM, VM),
         scratch_shapes=[pltpu.VMEM(x.shape, x.dtype) for x in (poses, codebook, offsets, conf, codes, kinds)]
         + [pltpu.SemaphoreType.DMA((NQ + 18,)), pltpu.SemaphoreType.DMA((6,))],
@@ -160,13 +161,12 @@
     return jnp.broadcast_to(row, (8, BS))
 
 
-def factor_block(block):
+def eliminate(upper_ref, inv_ref, first, last):
     groups = BS // 8
     row_ids = lax.broadcasted_iota(jnp.int32, (8, BS), 0)
-    lane_ids = lax.broadcasted_iota(jnp.int32, (8, BS), 1)
-    upper = [block[8 * g : 8 * g + 8, :] for g in range(groups)]
-    inv = [jnp.where(lane_ids == row_ids + 8 * g, 1.0, 0.0).astype(f32) for g in range(groups)]
-    for g in range(groups):
+    upper = {g: upper_ref[8 * g : 8 * g + 8, :] for g in range(first, groups)}
+    inv = {g: inv_ref[8 * g : 8 * g + 8, :] for g in range(first, groups)}
+    for g in range(first, last):
         k = 8 * g
         v, w = upper[g], inv[g]
         cols = [jnp.broadcast_to(v[:, k + j : k + j + 1], (8, BS)) for j in range(8)]
@@ -195,13 +195,9 @@
                 v = v - cols[j] * rows_v[j]
                 w = w - cols[j] * rows_w[j]
             upper[h], inv[h] = v, w
-    full = jnp.concatenate(upper, axis=0)
-    inverse = jnp.concatenate(inv, axis=0)
-    rr = lax.broadcasted_iota(jnp.int32, (BS, BS), 0)
-    cc = lax.broadcasted_iota(jnp.int32, (BS, BS), 1)
-    pivots = jnp.sum(jnp.where(rr == cc, full, 0.0), axis=1, keepdims=True)
-    scale = 1.0 / jnp.sqrt(pivots)
-    return jnp.where(cc >= rr, full * scale, 0.0), inverse * scale
+    for g in range(first, groups):
+        upper_ref[8 * g : 8 * g + 8, :] = upper[g]
+        inv_ref[8 * g : 8 * g + 8, :] = inv[g]
 
 
 def dot_nt(a, b):
@@ -215,13 +211,14 @@
 def exchange_kernel(
     mem, pat, scand, ccand, pg,
     x_hi, x_lo, diag, y_out, g_out,
-    s_all, low, inv, cur, fac_u, fac_i, raw, wh, wl,
-    s1r_a, s1r_b, s1, s2r_a, s2r_b, par, picked, other, both, mine, g1r, g1, g2r, g2, g3r,
+    s_all, low, inv, fac_u, fac_i, raw, wh, wl,
+    s1r_a, s1r_b, s1, s2r_a, s2r_b, par_a, par_b, picked, both_a, both_b, mine, g1r, g1, g2r, g2, g3r,
     snd_s1, rcv_s1, snd_s2, rcv_s2, snd_s3, rcv_s3, snd_sx, rcv_sx,
     snd_x, rcv_x, snd_a, rcv_a, snd_r2, snd_t2, snd_t1, rcv_r, rcv_t,
     snd_g1, rcv_g1, snd_g2, rcv_g2, snd_g4, rcv_g4, snd_g3, rcv_g3, snd_b, rcv_b, snd_r1,
 ):
     s1r, s2r = (s1r_a, s1r_b), (s2r_a, s2r_b)
+    par, both = (par_a, par_b), (both_a, both_b)
     f = lax.axis_index("frames")
     r = lax.axis_index("prow")
     c = lax.axis_index("pcol")
@@ -336,31 +333,82 @@
     def g4_copy(peer, at):
         return copy(g_out.at[at], g_out.at[at], snd_g4.at[peer], rcv_g4.at[at], (f, r, peer))
 
-    def a_copy(e, line, at):
+    def a_copy(k, e, line, at):
         return copy(
-            ccand.at[q_at(line, e)], par.at[at, e], snd_a.at[e, line], rcv_a.at[e, at], place(p, q_at(line, qh))
+            ccand.at[q_at(line, e), k], par[k].at[at, e],
+            snd_a.at[2 * k + e, line], rcv_a.at[2 * k + e, at], place(p, q_at(line, qh)),
         )
 
-    def b_copy():
-        return copy(picked.at[1 - qh], other, snd_b, rcv_b, place(p, q_at(ql, 1 - qh)))
-
-    def r1_copy(at):
-        return copy(mine, raw.at[f, f, at], snd_r1, rcv_r.at[at], place(p, q_at(ql, 1 - qh)))
-
-    def r2_copy(e, line, at):
-        part = raw.at[f, f, at]
-        return copy(part, part, snd_r2.at[e, line], rcv_r.at[at], place(p, q_at(line, qh)))
-
-    def t1_copy(e, at):
-        return copy(mine, raw.at[1 - f, f, at], snd_t1.at[e], rcv_t.at[at], place(p_at(ql, e), p))
-
-    def t2_copy(e, line, at):
-        part = raw.at[1 - f, f, at]
-        return copy(part, part, snd_t2.at[e, line], rcv_t.at[at], place(p_at(line, ph), q))
+    def b_copy(k):
+        return copy(
+            picked.at[k, 1 - qh], both[k].at[qh], snd_b.at[k], rcv_b.at[k], place(p, q_at(ql, 1 - qh))
+        )
+
+    def r1_copy(k, at):
+        return copy(
+            mine.at[k], raw.at[f, f, at, k], snd_r1.at[k], rcv_r.at[k, at], place(p, q_at(ql, 1 - qh))
+        )
+
+    def r2_copy(k, e, line, at):
+        part = raw.at[f, f, at, k]
+        return copy(part, part, snd_r2.at[2 * k + e, line], rcv_r.at[k, at], place(p, q_at(line, qh)))
+
+    def t1_copy(k, e, at):
+        return copy(
+            mine.at[k], raw.at[1 - f, f, at, k], snd_t1.at[k, e], rcv_t.at[k, at], place(p_at(ql, e), p)
+        )
+
+    def t2_copy(k, e, line, at):
+        part = raw.at[1 - f, f, at, k]
+        return copy(part, part, snd_t2.at[2 * k + e, line], rcv_t.at[k, at], place(p_at(line, ph), q))
 
     def x_copy(which, at, core):
         part = raw.at[which, core, at]
         return copy(part, part, snd_x.at[which, at], rcv_x.at[which, at], sibling)
+
+    def owner(k):
+        return q_parts(lax.rem(mem[f, k], 8))
+
+    def pick(k):
+        for e in range(2):
+            loop(1, 4, lambda d: a_copy(k, e, q_line(d), q_line(d)).wait())
+        for e in range(2):
+            picked[k, e] = par[k][owner(k)[0], e]
+        b_copy(k).start()
+
+    def spread_mine(k):
+        both[k][qh] = picked[k, qh]
+        b_copy(k).wait()
+
+        @pl.when(f == 0)
+        def _():
+            mine[k] = both[k][lax.rem(mem[0, k], 2)]
+
+        @pl.when(f == 1)
+        def _():
+            mine[k] = both[k][lax.rem(mem[1, k], 8) // 4].T
+
+        r1_copy(k, q).start()
+        for e in range(2):
+            away(p_at(ql, e), p, lambda: t1_copy(k, e, q).start())
+        raw[f, f, q, k] = mine[k]
+
+        @pl.when(jnp.logical_and(p == q, ql == pl_))
+        def _():
+            raw[1 - f, f, q, k] = mine[k]
+
+    def spread_on(k):
+        r1_copy(k, q_at(ql, 1 - qh)).wait_recv()
+        for e in range(2):
+            loop(1, 4, lambda d: r2_copy(k, e, q_line(d), q_at(ql, e)).start())
+        for e in range(2):
+            at = q_at(pl_, e)
+            away(q, at, lambda: t1_copy(k, e, at).wait_recv())
+            loop(1, 4, lambda d: t2_copy(k, e, p_line(d), at).start())
+        if k:
+            for e in range(2):
+                x_copy(f, q_at(ql, e), f).start()
+                x_copy(1 - f, q_at(pl_, e), f).start()
 
     for h in range(2):
         loop(1, 8, lambda d: s1_copy(h, q_peer(d), q).start())
@@ -369,7 +417,8 @@
         s1r[h][q] = scand[lo : lo + n, rows_of(q + 8 * f), :]
     g1r[c] = pg[c]
     for e in range(2):
-        par[ql, e] = ccand[q_at(ql, e)]
+        for k in range(2):
+            par[k][ql, e] = ccand[q_at(ql, e), k]
 
     for h in range(2):
         lo, n = CHUNKS[h]
@@ -386,9 +435,11 @@
     loop(1, 8, lambda d: g2_copy(r_peer(d), r).start())
     g2r[r] = g1[...]
 
-    for e in range(2):
-        loop(1, 4, lambda d: a_copy(e, q_line(d), ql).start())
-
+    for k in range(2):
+        for e in range(2):
+            loop(1, 4, lambda d: a_copy(k, e, q_line(d), ql).start())
+
+    pick(0)
     for h in range(2):
         lo, n = CHUNKS[h]
         loop(1, 8, lambda d: s2_copy(h, p_peer(d), p_peer(d)).wait())
@@ -398,6 +449,7 @@
             s_all[e, rows_of(q + 8 * f), :] = s2r[h][own_k + f * (own_m - own_k), e - lo]
         loop(1, 8, lambda d: s3_copy(h, q_peer(d), q).start())
         sx_copy(h, q, f).start()
+        pick(1) if h == 0 else spread_mine(0)
 
 
     loop(1, 8, lambda d: g2_copy(r_peer(d), r_peer(d)).wait())
@@ -436,7 +488,8 @@
         if k:
             lows = low[k, :, 0 : BS * k]
             value = value - dot_nt(lows, lows)
-        cur[...] = value
+        fac_u[...] = value
+        fac_i[...] = jnp.where(rr == cc, 1.0, 0.0)
 
     def after(k):
         at = slice(BS * k, BS * k + BS)
@@ -448,59 +501,11 @@
         diag[k] = lower
         if k == 0:
             pass_on(1)
-            spread_on()
+            spread_on(1)
         if k == 2:
             g3.wait()
             g_out[c] = g2[...] + g3r[...]
             loop(1, 8, lambda d: g4_copy(c_peer(d), c).start())
-
-    def owner(k):
-        return q_parts(lax.rem(mem[f, k], 8))
-
-    def pick():
-        for e in range(2):
-            loop(1, 4, lambda d: a_copy(e, q_line(d), q_line(d)).wait())
-        for e in range(2):
-            for k in range(2):
-                picked[e, k] = par[owner(k)[0], e, k]
-        b_copy().start()
-
-    def spread_mine():
-        b_copy().wait()
-        both[qh] = picked[qh]
-        both[1 - qh] = other[...]
-
-        @pl.when(f == 0)
-        def _():
-            for k in range(2):
-                mine[k] = both[lax.rem(mem[0, k], 2), k]
-
-        @pl.when(f == 1)
-        def _():
-            for k in range(2):
-                mine[k] = both[lax.rem(mem[1, k], 8) // 4, k].T
-
-        r1_copy(q).start()
-        for e in range(2):
-            away(p_at(ql, e), p, lambda: t1_copy(e, q).start())
-        raw[f, f, q] = mine[...]
-
-        @pl.when(jnp.logical_and(p == q, ql == pl_))
-        def _():
-            raw[1 - f, f, q] = mine[...]
-
-        x_copy(f, q, f).start()
-
-    def spread_on():
-        r1_copy(q_at(ql, 1 - qh)).wait_recv()
-        for e in range(2):
-            loop(1, 4, lambda d: r2_copy(e, q_line(d), q_at(ql, e)).start())
-        for e in range(2):
-            at = q_at(pl_, e)
-            away(q, at, lambda: t1_copy(e, at).wait_recv())
-            loop(1, 4, lambda d: t2_copy(e, p_line(d), at).start())
-            x_copy(1 - f, at, f).start()
-        x_copy(f, q_at(ql, 1 - qh), f).start()
 
     def step(k):
         for kk in range(STEPS):
@@ -508,26 +513,35 @@
             def _():
                 before(kk)
 
-        upper, inverse = factor_block(cur[...])
-        fac_u[...] = upper
-        fac_i[...] = inverse
+        eliminate(fac_u, fac_i, 0, 8)
+
+        @pl.when(k == 0)
+        def _():
+            spread_on(0)
+
+        eliminate(fac_u, fac_i, 8, 16)
+        pivots = jnp.sum(jnp.where(rr == cc, fac_u[...], 0.0), axis=1, keepdims=True)
+        scale = 1.0 / jnp.sqrt(pivots)
+        fac_u[...] = jnp.where(cc >= rr, fac_u[...] * scale, 0.0)
+        fac_i[...] = fac_i[...] * scale
         for kk in range(STEPS):
             @pl.when(k == kk)
             def _():
                 after(kk)
 
-    pick()
     pass_on(0)
-    spread_mine()
+    spread_mine(1)
     loop(0, STEPS, step)
 
     def arrives(d):
         for e in range(2):
             at = q_at(q_line(d), e)
-            r2_copy(e, q_line(d), at).wait_recv()
+            for k in range(2):
+                r2_copy(k, e, q_line(d), at).wait_recv()
             x_copy(f, at, f).start()
             at = q_at(p_line(d), e)
-            t2_copy(e, p_line(d), at).wait_recv()
+            for k in range(2):
+                t2_copy(k, e, p_line(d), at).wait_recv()
             x_copy(1 - f, at, f).start()
 
     loop(1, 4, arrives)
@@ -585,14 +599,16 @@
         g4_copy(c_peer(d), c).wait_send()
 
     loop(1, 8, tail)
-    r1_copy(q).wait_send()
-    for e in range(2):
-        away(p_at(ql, e), p, lambda: t1_copy(e, q).wait_send())
+    for k in range(2):
+        r1_copy(k, q).wait_send()
+        for e in range(2):
+            away(p_at(ql, e), p, lambda: t1_copy(k, e, q).wait_send())
 
     def tail_line(d):
-        for e in range(2):
-            r2_copy(e, q_line(d), q_at(ql, e)).wait_send()
-            t2_copy(e, p_line(d), q_at(pl_, e)).wait_send()
+        for k in range(2):
+            for e in range(2):
+                r2_copy(k, e, q_line(d), q_at(ql, e)).wait_send()
+                t2_copy(k, e, p_line(d), q_at(pl_, e)).wait_send()
 
     loop(1, 4, tail_line)
 
@@ -625,7 +641,6 @@
             vmem((WIDE, WIDE), f32),
             vmem((BS, BS), f32),
             vmem((BS, BS), f32),
-            vmem((BS, BS), f32),
             vmem((2, 2, 8, 2, BS, BS), f32),
             vmem((WIDE, WIDE), bf16),
             vmem((WIDE, WIDE), bf16),
@@ -634,10 +649,11 @@
             vmem((NQ, 8, BS), f32),
             vmem((8, CHUNKS[0][1], 8, BS), f32),
             vmem((8, CHUNKS[1][1], 8, BS), f32),
-            vmem((4, 2, 2, BS, BS), f32),
+            vmem((4, 2, BS, BS), f32),
+            vmem((4, 2, BS, BS), f32),
             vmem((2, 2, BS, BS), f32),
             vmem((2, BS, BS), f32),
-            vmem((2, 2, BS, BS), f32),
+            vmem((2, BS, BS), f32),
             vmem((2, BS, BS), f32),
             vmem((8, 8, BS), f32),
             vmem((8, BS), f32),
@@ -646,10 +662,12 @@
             vmem((8, BS), f32),
         ]
         + [sem((2, 8))] * 10
-        + [sem((2, 4))] * 4
-        + [sem((2,))]
-        + [sem((8,))] * 8
-        + [sem] * 5,
+        + [sem((4, 4))] * 4
+        + [sem((2, 2))]
+        + [sem((2, 8))] * 2
+        + [sem((8,))] * 6
+        + [sem] * 2
+        + [sem((2,))] * 3,
         compiler_params=pltpu.CompilerParams(
             collective_id=0, has_side_effects=True, vmem_limit_bytes=40 << 20
         ),

time: 98.7 us -> 92.4 us (0.936)
  Pallas kernels: 89.8 us -> 83.1 us
    pallas_call x1, Pallas kernels: 77.4 us -> 70.7 us  [exchange(): pl.pallas_call(exchange_kernel, out_shape=(jax.ShapeDtypeStruct((2, 1024,...]
where the time goes in v4:
time: 92.4 us; the launch traced here: 91.6 us
  Pallas kernels  83.1 us (90%)
  local copies, waits for them, and re-layouts  7.62 us (8%)
    pallas_call x1, Pallas kernels, exchange(): pl.pallas_call(exchange_kernel, out_shape=(jax.ShapeDtypeStruct((2, 1024,...  70.7 us
    pallas_call x1, Pallas kernels, update(): pl.pallas_call(update_kernel, out_shape=(jax.ShapeDtypeStruct(hess.shape,...  9.65 us
    unnamed x22, local copies, waits for them, and re-layouts  7.62 us
    pallas_call x1, Pallas kernels, prepare(): pl.pallas_call(prepare_kernel, out_shape=(jax.ShapeDtypeStruct((NQ, BS, B...  2.77 us

profile of v4, /device:TPU:105, one launch (start us, length us, event | category | flops | bytes accessed | tf_op | source)
XLA Modules:
  0.0 91.6 jit_solution(360515494021080317)
XLA Ops:
  0.6 0.0 copy-start.7
  0.6 0.0 copy-start
  0.7 2.2 %copy-done = f32[8,1,128,8,1,128]{5,4,3,2,1,0:T(1,128)S(1)} copy-done((f32[8,1,128,8,1,128]{5,4,3,2,1,0:T(1,128)S(1)}, f32[8,1,128,8,1,128]{5,4,3,2,1,0:T(1,128)}, u32[]{:S(2)}) %copy-start) | copy-done | bytes 4194328
  2.8 0.0 copy-start.2
  2.8 1.2 %copy-done.2 = bf16[2048,256]{1,0:T(8,128)(2,1)S(1)} copy-done((bf16[2048,256]{1,0:T(8,128)(2,1)S(1)}, bf16[2048,256]{1,0:T(8,128)(2,1)}, u32[]{:S(2)}) %copy-start.2) | copy-done | bytes 1048600
  4.1 0.0 copy-start.4
  4.1 0.7 copy-done.4
  4.8 0.0 copy-start.5
  4.8 0.7 copy-done.5
  5.5 0.0 copy-start.6
  5.5 0.7 copy-done.6
  6.2 0.0 copy-start.8
  6.2 0.7 copy-done.8
  6.9 0.0 copy-start.9
  6.9 0.7 copy-done.9
  7.6 0.0 copy-start.10
  7.6 0.7 copy-done.10
  8.3 0.0 copy-start.3
  8.3 0.0 copy-start.1
  8.3 2.8 %prepare.1 = (f32[10,128,128]{2,1,0:T(8,128)S(1)}, f32[8,2,128,128]{3,2,1,0:T(8,128)S(1)}, f32[64,128]{1,0:T(8,128)S(1)}) custom-call(s32[2,2]{1,0:T(2,128)S(1)} %copy-done.6, f32[8,128,8,1,128]{4,3,2,1,0:T(1,128)S(1)} %bitcast.12, bf16[2048,256]{1,0:T(8,128)(2,1)S(1)} %copy-done.2, bf16[32,256]{1,0:T(8,128)(2,1)S(1)} %copy-done.4, ...), custom_call_target="tpu_custom_call" | custom-call | tf_op jit(solution)/shard_map/prepare/pallas_call | solution.py:144
  11.1 0.0 copy-done.7
  11.1 0.0 copy-done.3
  11.1 70.7 %exchange.1 = (bf16[2,1024,512]{2,1,0:T(8,128)(2,1)S(1)}, bf16[2,1024,512]{2,1,0:T(8,128)(2,1)S(1)}, f32[4,128,128]{2,1,0:T(8,128)S(1)}, f32[8,512]{1,0:T(8,128)S(1)}, f32[8,8,128]{2,1,0:T(8,128)S(1)}) custom-call(s32[2,2]{1,0:T(2,128)S(1)} %copy-done.7, s32[64,64]{1,0:T(8,128)S(1)} %copy-done.3, f32[10,128,128]{2,1,0:T(8,128)S(1)} %get-tuple-element.12.scand, ...), custom_call_target="tpu_custom_call" | custom-call | tf_op jit(solution)/shard_map/exchange/pallas_call | solution.py:627
  81.7 0.0 copy-done.1
  81.7 9.7 %update.1 = (f32[8,1024,128]{2,1,0:T(8,128)}, f32[8,128]{1,0:T(8,128)}) custom-call(s32[2,2]{1,0:T(2,128)S(1)} %copy-done.7, s32[64,64]{1,0:T(8,128)S(1)} %copy-done.3, f32[4,128,128]{2,1,0:T(8,128)S(1)} %get-tuple-element.15.diag, bf16[2,1024,512]{2,1,0:T(8,128)(2,1)S(1)} %get-tuple-element.16.x_hi, bf16[2,1024,512]{2,1,0:T(8,128)(2,1)S(1)} %get-tuple-element.17.x_lo, ...), custom_call_target="tpu_custom_call" | custom-call | tf_op jit(solution)/shard_map/update/pallas_call | solution.py:749
Async XLA Ops:
  0.6 10.4 %copy-start.7 = (s32[2,2]{1,0:T(2,128)S(1)}, s32[2,2]{1,0:T(2,128)}, u32[]{:S(2)}) copy-start(s32[2,2]{1,0:T(2,128)} %mem.5) | copy-start | bytes 52
  0.6 2.2 %copy-start = (f32[8,1,128,8,1,128]{5,4,3,2,1,0:T(1,128)S(1)}, f32[8,1,128,8,1,128]{5,4,3,2,1,0:T(1,128)}, u32[]{:S(2)}) copy-start(f32[8,1,128,8,1,128]{5,4,3,2,1,0:T(1,128)} %param.15) | copy-start | bytes 12582916
  2.8 1.2 %copy-start.2 = (bf16[2048,256]{1,0:T(8,128)(2,1)S(1)}, bf16[2048,256]{1,0:T(8,128)(2,1)}, u32[]{:S(2)}) copy-start(bf16[2048,256]{1,0:T(8,128)(2,1)} %poses_at.1) | copy-start | bytes 3145732
  4.1 0.7 copy-start.4
  4.8 0.7 copy-start.5
  5.5 0.7 copy-start.6
  6.2 0.7 copy-start.8
  6.9 0.7 copy-start.9
  7.6 0.7 copy-start.10
  8.3 2.8 %copy-start.3 = (s32[64,64]{1,0:T(8,128)S(1)}, s32[64,64]{1,0:T(8,128)}, u32[]{:S(2)}) copy-start(s32[64,64]{1,0:T(8,128)} %pat.3) | copy-start | bytes 49156
  8.3 73.5 %copy-start.1 = (f32[8,1,128,8,1,128]{5,4,3,2,1,0:T(1,128)S(1)}, f32[8,1,128,8,1,128]{5,4,3,2,1,0:T(1,128)}, u32[]{:S(2)}) copy-start(f32[8,1,128,8,1,128]{5,4,3,2,1,0:T(1,128)} %param.15) | copy-start | bytes 12582916

commit v5 on v4

--- a/solution.py
+++ b/solution.py
@@ -154,7 +154,13 @@
         + [pltpu.SemaphoreType.DMA((NQ + 18,)), pltpu.SemaphoreType.DMA((6,))],
         compiler_params=pltpu.CompilerParams(vmem_limit_bytes=24 << 20),
         name="prepare",
-    )(mem, hess, poses, codebook, offsets, conf, codes, kinds)
+    )(
+        mem,
+        *(
+            pltpu.with_memory_space_constraint(x, pltpu.HBM)
+            for x in (hess, poses, codebook, offsets, conf, codes, kinds)
+        ),
+    )
 
 
 def spread(row):
@@ -439,7 +445,6 @@
         for e in range(2):
             loop(1, 4, lambda d: a_copy(k, e, q_line(d), ql).start())
 
-    pick(0)
     for h in range(2):
         lo, n = CHUNKS[h]
         loop(1, 8, lambda d: s2_copy(h, p_peer(d), p_peer(d)).wait())
@@ -449,7 +454,6 @@
             s_all[e, rows_of(q + 8 * f), :] = s2r[h][own_k + f * (own_m - own_k), e - lo]
         loop(1, 8, lambda d: s3_copy(h, q_peer(d), q).start())
         sx_copy(h, q, f).start()
-        pick(1) if h == 0 else spread_mine(0)
 
 
     loop(1, 8, lambda d: g2_copy(r_peer(d), r_peer(d)).wait())
@@ -501,6 +505,7 @@
         diag[k] = lower
         if k == 0:
             pass_on(1)
+        if k == 1:
             spread_on(1)
         if k == 2:
             g3.wait()
@@ -516,6 +521,11 @@
         eliminate(fac_u, fac_i, 0, 8)
 
         @pl.when(k == 0)
+        def _():
+            spread_mine(0)
+            spread_mine(1)
+
+        @pl.when(k == 1)
         def _():
             spread_on(0)
 
@@ -529,8 +539,9 @@
             def _():
                 after(kk)
 
+    pick(0)
+    pick(1)
     pass_on(0)
-    spread_mine(1)
     loop(0, STEPS, step)
 
     def arrives(d):

time: 92.4 us -> 87.1 us (0.943)
  local copies, waits for them, and re-layouts: 7.62 us -> 0.83 us
  Pallas kernels: 83.1 us -> 85.5 us
    unnamed x22 -> x8, local copies, waits for them, and re-layouts: 7.62 us -> 0.83 us
    pallas_call x1, Pallas kernels: 70.7 us -> 72.8 us  [exchange(): pl.pallas_call(exchange_kernel, out_shape=(jax.ShapeDtypeStruct((2, 1024,...]
where the time goes in v5:
time: 87.1 us; the launch traced here: 87 us
  Pallas kernels  85.5 us (98%)
    pallas_call x1, Pallas kernels, exchange(): pl.pallas_call(exchange_kernel, out_shape=(jax.ShapeDtypeStruct((2, 1024,...  72.8 us
    pallas_call x1, Pallas kernels, update(): pl.pallas_call(update_kernel, out_shape=(jax.ShapeDtypeStruct(hess.shape,...  9.82 us
    pallas_call x1, Pallas kernels, prepare(): pl.pallas_call(prepare_kernel, out_shape=(jax.ShapeDtypeStruct((NQ, BS, B...  2.88 us

profile of v5, /device:TPU:105, one launch (start us, length us, event | category | flops | bytes accessed | tf_op | source)
XLA Modules:
  0.0 87.0 jit_solution(13987147826283279006)
XLA Ops:
  0.6 0.0 copy-start.1
  0.6 0.0 copy-start
  0.7 0.0 copy-start.2
  0.7 0.8 copy-done.2
  1.5 0.0 copy-start.3
  1.5 2.9 %prepare.1 = (f32[10,128,128]{2,1,0:T(8,128)S(1)}, f32[8,2,128,128]{3,2,1,0:T(8,128)S(1)}, f32[64,128]{1,0:T(8,128)S(1)}) custom-call(s32[2,2]{1,0:T(2,128)S(1)} %copy-done.2, f32[8,128,8,1,128]{4,3,2,1,0:T(1,128)} %bitcast.12, bf16[2048,256]{1,0:T(8,128)(2,1)} %poses_at.1, bf16[32,256]{1,0:T(8,128)(2,1)} %codebook_at.1, bf16[32,256]{1,0:T(8,128)(2,1)} %offsets_at.1, ...), custom_call_target="tpu_custom_call" | custom-call | tf_op jit(solution)/shard_map/prepare/pallas_call | solution.py:144
  4.4 0.0 copy-done.1
  4.4 0.0 copy-done.3
  4.4 72.8 %exchange.1 = (bf16[2,1024,512]{2,1,0:T(8,128)(2,1)S(1)}, bf16[2,1024,512]{2,1,0:T(8,128)(2,1)S(1)}, f32[4,128,128]{2,1,0:T(8,128)S(1)}, f32[8,512]{1,0:T(8,128)S(1)}, f32[8,8,128]{2,1,0:T(8,128)S(1)}) custom-call(s32[2,2]{1,0:T(2,128)S(1)} %copy-done.3, s32[64,64]{1,0:T(8,128)S(1)} %copy-done.1, f32[10,128,128]{2,1,0:T(8,128)S(1)} %get-tuple-element.12.scand, ...), custom_call_target="tpu_custom_call" | custom-call | tf_op jit(solution)/shard_map/exchange/pallas_call | solution.py:638
  77.2 0.0 copy-done
  77.2 9.8 %update.1 = (f32[8,1024,128]{2,1,0:T(8,128)}, f32[8,128]{1,0:T(8,128)}) custom-call(s32[2,2]{1,0:T(2,128)S(1)} %copy-done.3, s32[64,64]{1,0:T(8,128)S(1)} %copy-done.1, f32[4,128,128]{2,1,0:T(8,128)S(1)} %get-tuple-element.15.diag, bf16[2,1024,512]{2,1,0:T(8,128)(2,1)S(1)} %get-tuple-element.16.x_hi, bf16[2,1024,512]{2,1,0:T(8,128)(2,1)S(1)} %get-tuple-element.17.x_lo, ...), custom_call_target="tpu_custom_call" | custom-call | tf_op jit(solution)/shard_map/update/pallas_call | solution.py:760
Async XLA Ops:
  0.6 3.7 %copy-start.1 = (s32[64,64]{1,0:T(8,128)S(1)}, s32[64,64]{1,0:T(8,128)}, u32[]{:S(2)}) copy-start(s32[64,64]{1,0:T(8,128)} %pat.3) | copy-start | bytes 49156
  0.6 76.5 %copy-start = (f32[8,1,128,8,1,128]{5,4,3,2,1,0:T(1,128)S(1)}, f32[8,1,128,8,1,128]{5,4,3,2,1,0:T(1,128)}, u32[]{:S(2)}) copy-start(f32[8,1,128,8,1,128]{5,4,3,2,1,0:T(1,128)} %param.15) | copy-start | bytes 12582916
  0.7 0.8 copy-start.2
  1.5 2.9 %copy-start.3 = (s32[2,2]{1,0:T(2,128)S(1)}, s32[2,2]{1,0:T(2,128)}, u32[]{:S(2)}) copy-start(s32[2,2]{1,0:T(2,128)} %mem.5) | copy-start | bytes 52

commit v6 on v5

--- a/solution.py
+++ b/solution.py
@@ -54,51 +54,7 @@
 HBM = pl.BlockSpec(memory_space=pltpu.HBM)
 
 
-def prepare_kernel(
-    mem, hess, poses_at, codebook_at, offsets_at, conf_at, codes_at, kinds_at, scand, ccand, pg,
-    poses, codebook, offsets, conf, codes, kinds, sem, in_sem,
-):
-    fetches = [
-        pltpu.make_async_copy(src, dst, in_sem.at[n])
-        for n, (src, dst) in enumerate(
-            [
-                (codes_at, codes), (conf_at, conf), (kinds_at, kinds),
-                (poses_at, poses), (codebook_at, codebook), (offsets_at, offsets),
-            ]
-        )
-    ]
-    for fetch in fetches:
-        fetch.start()
-    f = lax.axis_index("frames")
-    slot = [member(mem, k) // 8 for k in range(STEPS)]
-    copies = [
-        pltpu.make_async_copy(hess.at[slot[k], :, slot[m], 0, :], scand.at[q], sem.at[q])
-        for q, (k, m) in enumerate(PAIRS)
-    ]
-    for copy in copies:
-        copy.start()
-    by_col = [
-        pltpu.make_async_copy(hess.at[:, :, slot[k], 0, :], ccand.at[:, k], sem.at[NQ + k])
-        for k in range(2)
-    ]
-    by_row = [
-        pltpu.make_async_copy(hess.at[slot[2 + k], :, b, 0, :], ccand.at[b, k], sem.at[NQ + 2 + 8 * k + b])
-        for k in range(2)
-        for b in range(8)
-    ]
-
-    @pl.when(f == 0)
-    def _():
-        for copy in by_col:
-            copy.start()
-
-    @pl.when(f == 1)
-    def _():
-        for copy in by_row:
-            copy.start()
-
-    for fetch in fetches:
-        fetch.wait()
+def moments(poses, codebook, offsets, conf, codes, kinds):
     ids = lax.broadcasted_iota(jnp.int32, (CODES, BS), 0)
     weights, marks = [], []
     for s in range(16):
@@ -122,45 +78,7 @@
     moment = moment - lax.dot_general(
         pair, offsets[...].astype(f32), NN, precision=precise, preferred_element_type=f32
     )
-    moment = moment / math.sqrt(FRAMES / CODES)
-    for half in range(2):
-        pg[pl.ds(half, CODES, stride=2), :] = moment[:, BS * half : BS * half + BS]
-
-    for copy in copies:
-        copy.wait()
-
-    @pl.when(f == 0)
-    def _():
-        for copy in by_col:
-            copy.wait()
-
-    @pl.when(f == 1)
-    def _():
-        for copy in by_row:
-            copy.wait()
-
-
-def prepare(mem, hess, poses, codebook, offsets, conf, codes, kinds):
-    return pl.pallas_call(
-        prepare_kernel,
-        out_shape=(
-            jax.ShapeDtypeStruct((NQ, BS, BS), f32),
-            jax.ShapeDtypeStruct((8, 2, BS, BS), f32),
-            jax.ShapeDtypeStruct((64, BS), f32),
-        ),
-        in_specs=[SM] + [HBM] * 7,
-        out_specs=(VM, VM, VM),
-        scratch_shapes=[pltpu.VMEM(x.shape, x.dtype) for x in (poses, codebook, offsets, conf, codes, kinds)]
-        + [pltpu.SemaphoreType.DMA((NQ + 18,)), pltpu.SemaphoreType.DMA((6,))],
-        compiler_params=pltpu.CompilerParams(vmem_limit_bytes=24 << 20),
-        name="prepare",
-    )(
-        mem,
-        *(
-            pltpu.with_memory_space_constraint(x, pltpu.HBM)
-            for x in (hess, poses, codebook, offsets, conf, codes, kinds)
-        ),
-    )
+    return moment / math.sqrt(FRAMES / CODES)
 
 
 def spread(row):
@@ -215,14 +133,25 @@
 
 
 def exchange_kernel(
-    mem, pat, scand, ccand, pg,
-    x_hi, x_lo, diag, y_out, g_out,
-    s_all, low, inv, fac_u, fac_i, raw, wh, wl,
+    mem, pat, hess_at, poses_at, codebook_at, offsets_at, conf_at, codes_at, kinds_at,
+    x_row, x_col, diag, y_out, g_out,
+    hess, poses, codebook, offsets, conf, codes, kinds, scand, ccand, pg, s_all, low, inv, fac_u, fac_i, raw, wh, wl,
     s1r_a, s1r_b, s1, s2r_a, s2r_b, par_a, par_b, picked, both_a, both_b, mine, g1r, g1, g2r, g2, g3r,
     snd_s1, rcv_s1, snd_s2, rcv_s2, snd_s3, rcv_s3, snd_sx, rcv_sx,
     snd_x, rcv_x, snd_a, rcv_a, snd_r2, snd_t2, snd_t1, rcv_r, rcv_t,
-    snd_g1, rcv_g1, snd_g2, rcv_g2, snd_g4, rcv_g4, snd_g3, rcv_g3, snd_b, rcv_b, snd_r1,
+    snd_g1, rcv_g1, snd_g2, rcv_g2, snd_g4, rcv_g4, snd_g3, rcv_g3, snd_b, rcv_b, snd_r1, in_sem,
 ):
+    fetches = [
+        pltpu.make_async_copy(src, dst, in_sem.at[n])
+        for n, (src, dst) in enumerate(
+            [
+                (hess_at, hess), (codes_at, codes), (conf_at, conf), (kinds_at, kinds),
+                (poses_at, poses), (codebook_at, codebook), (offsets_at, offsets),
+            ]
+        )
+    ]
+    for fetch in fetches:
+        fetch.start()
     s1r, s2r = (s1r_a, s1r_b), (s2r_a, s2r_b)
     par, both = (par_a, par_b), (both_a, both_b)
     f = lax.axis_index("frames")
@@ -301,6 +230,24 @@
 
     loop(0, 2, greet_turn)
     same = jnp.where(jnp.logical_and(p == q, ql == pl_), 1, 0)
+
+    slot = [member(mem, k) // 8 for k in range(STEPS)]
+    fetches[0].wait()
+    for e, (k, m) in enumerate(PAIRS):
+        scand[e] = hess[slot[k], pl.ds(slot[m], BS, stride=8), :]
+
+    @pl.when(f == 0)
+    def _():
+        for k in range(2):
+            for v in range(8):
+                ccand[v, k] = hess[v, pl.ds(slot[k], BS, stride=8), :]
+
+    @pl.when(f == 1)
+    def _():
+        for k in range(2):
+            for v in range(8):
+                ccand[v, k] = hess[slot[2 + k], pl.ds(v, BS, stride=8), :]
+
     pl.semaphore_wait(barrier, 19 - 2 * same)
 
     def rows_of(slice_id):
@@ -331,7 +278,7 @@
         return copy(part, part, snd_sx.at[h, at], rcv_sx.at[h, at], sibling)
 
     def g1_copy(peer, at):
-        return copy(pg.at[peer], g1r.at[at], snd_g1.at[peer], rcv_g1.at[at], (f, r, peer))
+        return copy(pg.at[rows_of(peer)], g1r.at[at], snd_g1.at[peer], rcv_g1.at[at], (f, r, peer))
 
     def g2_copy(peer, at):
         return copy(g1, g2r.at[at], snd_g2.at[peer], rcv_g2.at[at], (f, peer, c))
@@ -418,13 +365,21 @@
 
     for h in range(2):
         loop(1, 8, lambda d: s1_copy(h, q_peer(d), q).start())
-    loop(1, 8, lambda d: g1_copy(c_peer(d), c).start())
+    for k in range(2):
+        for e in range(2):
+            loop(1, 4, lambda d: a_copy(k, e, q_line(d), ql).start())
     for h, (lo, n) in enumerate(CHUNKS):
         s1r[h][q] = scand[lo : lo + n, rows_of(q + 8 * f), :]
-    g1r[c] = pg[c]
     for e in range(2):
         for k in range(2):
             par[k][ql, e] = ccand[q_at(ql, e), k]
+    for fetch in fetches[1:]:
+        fetch.wait()
+    moment = moments(poses, codebook, offsets, conf, codes, kinds)
+    for half in range(2):
+        pg[pl.ds(half, CODES, stride=2), :] = moment[:, BS * half : BS * half + BS]
+    loop(1, 8, lambda d: g1_copy(c_peer(d), c).start())
+    g1r[c] = pg[rows_of(c), :]
 
     for h in range(2):
         lo, n = CHUNKS[h]
@@ -441,9 +396,6 @@
     loop(1, 8, lambda d: g2_copy(r_peer(d), r).start())
     g2r[r] = g1[...]
 
-    for k in range(2):
-        for e in range(2):
-            loop(1, 4, lambda d: a_copy(k, e, q_line(d), ql).start())
 
     for h in range(2):
         lo, n = CHUNKS[h]
@@ -481,12 +433,15 @@
             sx_ready(0)
         if k == 2:
             sx_ready(1)
-        for m in range(k):
-            keep = pat[member(mem, k), member(mem, m)].astype(f32)
-            value = s_all[PAIRS.index((k, m))] * keep
-            if m:
-                value = value - keep * dot_nt(low[k, :, 0 : BS * m], low[m, :, 0 : BS * m])
-            low[k, :, BS * m : BS * m + BS] = dot_nt(value, inv[BS * m : BS * m + BS, BS * m : BS * m + BS])
+        if k:
+            row = jnp.concatenate(
+                [
+                    s_all[PAIRS.index((k, m))] * pat[member(mem, k), member(mem, m)].astype(f32)
+                    for m in range(k)
+                ],
+                axis=1,
+            )
+            low[k, :, 0 : BS * k] = dot_nt(row, inv[0 : BS * k, 0 : BS * k])
         value = s_all[PAIRS.index((k, k))] * pat[member(mem, k), member(mem, k)].astype(f32)
         value = value + jnp.where(rr == cc, SHIFT, 0.0)
         if k:
@@ -572,6 +527,14 @@
     gp = jnp.broadcast_to(gp, (16, WIDE))
     y_out[...] = dot3(split(gp), (wh[...], wl[...]))[0:8]
 
+    def store(which, rows, at, x):
+        hi, rest = split(x)
+        for target, parts in ((x_row, (hi, rest, hi)), (x_col, (hi, hi, rest))):
+            @pl.when(which == (1 if target is x_col else 0))
+            def _():
+                for n, part in enumerate(parts):
+                    target[rows, WIDE * n + at : WIDE * n + at + half] = part
+
     def panel(which, t):
         base = r + which * (c - r)
         ones, twos, keeps = [], [], []
@@ -594,13 +557,9 @@
         two = split(jnp.concatenate(twos, axis=0))
         second = dot3(one, w21) + dot3(two, w22)
         rows = pl.ds(pl.multiple_of(half * t, half), half)
-        hi, rest = split(dot3(one, w11))
-        x_hi[which, rows, 0:half] = hi
-        x_lo[which, rows, 0:half] = rest
+        store(which, rows, 0, dot3(one, w11))
         second = jnp.concatenate([second[0:BS] * keeps[0], second[BS:half] * keeps[1]], axis=0)
-        hi, rest = split(second)
-        x_hi[which, rows, half:WIDE] = hi
-        x_lo[which, rows, half:WIDE] = rest
+        store(which, rows, half, second)
 
     loop(0, 8, lambda t: panel(t // 4, lax.rem(t, 4)))
 
@@ -632,21 +591,25 @@
     loop(0, 8, tail_pair)
 
 
-def exchange(mem, pat, scand, ccand, pg):
+def exchange(mem, pat, *operands):
     vmem = pltpu.VMEM
     sem = pltpu.SemaphoreType.DMA
     return pl.pallas_call(
         exchange_kernel,
         out_shape=(
-            jax.ShapeDtypeStruct((2, 1024, WIDE), bf16),
-            jax.ShapeDtypeStruct((2, 1024, WIDE), bf16),
+            jax.ShapeDtypeStruct((1024, 3 * WIDE), bf16),
+            jax.ShapeDtypeStruct((1024, 3 * WIDE), bf16),
             jax.ShapeDtypeStruct((STEPS, BS, BS), f32),
             jax.ShapeDtypeStruct((8, WIDE), f32),
             jax.ShapeDtypeStruct((8, 8, BS), f32),
         ),
-        in_specs=[SM, SM, VM, VM, VM],
+        in_specs=[SM, SM] + [HBM] * 7,
         out_specs=(VM,) * 5,
-        scratch_shapes=[
+        scratch_shapes=[vmem(x.shape, x.dtype) for x in operands]
+        + [
+            vmem((NQ, BS, BS), f32),
+            vmem((8, 2, BS, BS), f32),
+            vmem((64, BS), f32),
             vmem((NQ, BS, BS), f32),
             vmem((STEPS, BS, WIDE), f32),
             vmem((WIDE, WIDE), f32),
@@ -678,15 +641,16 @@
         + [sem((2, 8))] * 2
         + [sem((8,))] * 6
         + [sem] * 2
-        + [sem((2,))] * 3,
+        + [sem((2,))] * 3
+        + [sem((7,))],
         compiler_params=pltpu.CompilerParams(
             collective_id=0, has_side_effects=True, vmem_limit_bytes=40 << 20
         ),
         name="exchange",
-    )(mem, pat, scand, ccand, pg)
-
-
-def update_kernel(mem, pat, diag, x_hi, x_lo, y, g, hess, out, grad_out, rows, in_sem, out_sem):
+    )(mem, pat, *(pltpu.with_memory_space_constraint(x, pltpu.HBM) for x in operands))
+
+
+def update_kernel(mem, pat, diag, x_row, x_col, y, g, hess, out, grad_out, rows, in_sem, out_sem):
     r = lax.axis_index("prow")
     c = lax.axis_index("pcol")
 
@@ -705,7 +669,7 @@
             pivot = jnp.logical_or(pivot, i == member(mem, k))
         return pivot
 
-    dec = dot3(split(jnp.concatenate([y[...], y[...]], axis=0)), (x_hi[0], x_lo[0]))
+    dec = dot3(split(jnp.concatenate([y[...], y[...]], axis=0)), (x_row[:, 0:WIDE], x_row[:, WIDE : 2 * WIDE]))
     for a in range(8):
         i = 8 * a + r
         val = g[a, pl.ds(r, 1), :] - dec[0:1, BS * a : BS * a + BS]
@@ -716,11 +680,10 @@
     rr = lax.broadcasted_iota(jnp.int32, (BS, BS), 0)
     cc = lax.broadcasted_iota(jnp.int32, (BS, BS), 1)
     shift = jnp.where(rr == cc, SHIFT, 0.0)
-    cols = (x_hi[1], x_lo[1])
 
     def two_rows(t):
         at = pl.ds(pl.multiple_of(2 * BS * t, 2 * BS), 2 * BS)
-        upd = dot3((x_hi[0, at, :], x_lo[0, at, :]), cols)
+        upd = lax.dot_general(x_row[at, :], x_col[...], NT, preferred_element_type=f32)
         for e in range(2):
             a = 2 * t + e
             i = 8 * a + r
@@ -741,10 +704,11 @@
                     there = pl.ds(pk // 8, BS, stride=8)
                     mine = pl.ds(pl.multiple_of(BS * a, BS), BS)
                     part = slice(BS * k, BS * k + BS)
+                    rest = slice(WIDE + BS * k, WIDE + BS * k + BS)
 
                     @pl.when(i != pk)
                     def _():
-                        rows[a, there, :] = x_hi[0, mine, part].astype(f32) + x_lo[0, mine, part].astype(f32)
+                        rows[a, there, :] = x_row[mine, part].astype(f32) + x_row[mine, rest].astype(f32)
 
                     @pl.when(i == pk)
                     def _():
@@ -756,7 +720,7 @@
         save(a).wait()
 
 
-def update(mem, pat, diag, x_hi, x_lo, y, g, hess):
+def update(mem, pat, diag, x_row, x_col, y, g, hess):
     return pl.pallas_call(
         update_kernel,
         out_shape=(
@@ -772,20 +736,18 @@
         ],
         compiler_params=pltpu.CompilerParams(vmem_limit_bytes=32 << 20),
         name="update",
-    )(mem, pat, diag, x_hi, x_lo, y, g, hess)
+    )(mem, pat, diag, x_row, x_col, y, g, hess)
 
 
 def shards(
     poses, codebook, offsets, confidence, code_ids, creature_ids, hess_raw, pattern, membership
 ):
-    scand, ccand, pg = prepare(
-        membership, hess_raw.reshape(8, BS, 8, 1, BS), poses, codebook, offsets,
+    hess = hess_raw.reshape(8, 1024, BS)
+    x_row, x_col, diag, y, g = exchange(
+        membership, pattern, hess, poses, codebook, offsets,
         confidence.reshape(16, BS), code_ids.reshape(16, BS), creature_ids.reshape(16, BS),
     )
-    x_hi, x_lo, diag, y, g = exchange(membership, pattern, scand, ccand, pg.reshape(8, 8, BS))
-    state, grad = update(
-        membership, pattern, diag, x_hi, x_lo, y, g, hess_raw.reshape(8, 1024, BS)
-    )
+    state, grad = update(membership, pattern, diag, x_row, x_col, y, g, hess)
     return state.reshape(hess_raw.shape), grad.reshape(8, 1, BS)
 
 

time: 87.1 us -> 86.8 us (level)
  Pallas kernels: 85.5 us -> 84.2 us
  local copies, waits for them, and re-layouts: 0.83 us -> 1.8 us
    pallas_call x2 -> x1, Pallas kernels: 75.7 us -> 74.6 us  [exchange(): pl.pallas_call(exchange_kernel, out_shape=(jax.ShapeDtypeStruct((1024, 3...]
    unnamed x8 -> x6, local copies, waits for them, and re-layouts: 0.83 us -> 1.8 us
where the time goes in v6:
time: 86.8 us; the launch traced here: 86.7 us
  Pallas kernels  84.2 us (97%)
  local copies, waits for them, and re-layouts  1.8 us (2%)
    pallas_call x1, Pallas kernels, exchange(): pl.pallas_call(exchange_kernel, out_shape=(jax.ShapeDtypeStruct((1024, 3...  74.6 us
    pallas_call x1, Pallas kernels, update(): pl.pallas_call(update_kernel, out_shape=(jax.ShapeDtypeStruct(hess.shape,...  9.61 us
    unnamed x6, local copies, waits for them, and re-layouts  1.8 us

profile of v6, /device:TPU:105, one launch (start us, length us, event | category | flops | bytes accessed | tf_op | source)
XLA Modules:
  0.0 86.7 jit_solution(2803280383669962574)
XLA Ops:
  0.6 0.0 copy-start
  0.6 0.0 copy-start.1
  0.7 0.9 %copy-done.1 = s32[64,64]{1,0:T(8,128)S(1)} copy-done((s32[64,64]{1,0:T(8,128)S(1)}, s32[64,64]{1,0:T(8,128)}, u32[]{:S(2)}) %copy-start.1) | copy-done | bytes 16408
  1.6 0.0 copy-start.2
  1.6 0.9 %copy-done.2 = s32[2,2]{1,0:T(2,128)S(1)} copy-done((s32[2,2]{1,0:T(2,128)S(1)}, s32[2,2]{1,0:T(2,128)}, u32[]{:S(2)}) %copy-start.2) | copy-done | bytes 40
  2.5 74.6 %exchange.1 = (bf16[1024,1536]{1,0:T(8,128)(2,1)S(1)}, bf16[1024,1536]{1,0:T(8,128)(2,1)S(1)}, f32[4,128,128]{2,1,0:T(8,128)S(1)}, f32[8,512]{1,0:T(8,128)S(1)}, f32[8,8,128]{2,1,0:T(8,128)S(1)}) custom-call(s32[2,2]{1,0:T(2,128)S(1)} %copy-done.2, s32[64,64]{1,0:T(8,128)S(1)} %copy-done.1, f32[8,1024,128]{2,1,0:T(8,128)} %bitcast.10, ...), custom_call_target="tpu_custom_call" | custom-call | tf_op jit(solution)/shard_map/exchange/pallas_call | solution.py:597
  77.1 0.0 copy-done
  77.1 9.6 %update.1 = (f32[8,1024,128]{2,1,0:T(8,128)}, f32[8,128]{1,0:T(8,128)}) custom-call(s32[2,2]{1,0:T(2,128)S(1)} %copy-done.2, s32[64,64]{1,0:T(8,128)S(1)} %copy-done.1, f32[4,128,128]{2,1,0:T(8,128)S(1)} %get-tuple-element.9.diag, bf16[1024,1536]{1,0:T(8,128)(2,1)S(1)} %get-tuple-element.10.x_row, bf16[1024,1536]{1,0:T(8,128)(2,1)S(1)} %get-tuple-element.11.x_col, ...), custom_call_target="tpu_custom_call" | custom-call | tf_op jit(solution)/shard_map/update/pallas_call | solution.py:724
Async XLA Ops:
  0.6 76.5 %copy-start = (f32[8,1,128,8,1,128]{5,4,3,2,1,0:T(1,128)S(1)}, f32[8,1,128,8,1,128]{5,4,3,2,1,0:T(1,128)}, u32[]{:S(2)}) copy-start(f32[8,1,128,8,1,128]{5,4,3,2,1,0:T(1,128)} %param.15) | copy-start | bytes 12582916
  0.6 0.9 %copy-start.1 = (s32[64,64]{1,0:T(8,128)S(1)}, s32[64,64]{1,0:T(8,128)}, u32[]{:S(2)}) copy-start(s32[64,64]{1,0:T(8,128)} %pat.3) | copy-start | bytes 49156
  1.6 0.9 %copy-start.2 = (s32[2,2]{1,0:T(2,128)S(1)}, s32[2,2]{1,0:T(2,128)}, u32[]{:S(2)}) copy-start(s32[2,2]{1,0:T(2,128)} %mem.3) | copy-start | bytes 52

commit v7 on v6

--- a/solution.py
+++ b/solution.py
@@ -180,6 +180,11 @@
     ql, qh = q_parts(q)
     pl_, ph = p_parts(p)
 
+    hub = lax.rem(pl_ + ql, 4)
+
+    def turn(v):
+        return lax.rem(v - p_parts(q)[0] + 4, 4)
+
     def q_line(d):
         return lax.rem(ql + d, 4)
 
@@ -225,11 +230,11 @@
             fn()
 
     def greet_turn(e):
-        away(p_at(ql, e), p, lambda: greet(place(p_at(ql, e), p)))
-        away(q, q_at(pl_, e), lambda: greet(place(q, q_at(pl_, e))))
+        away(p_at(hub, e), p, lambda: greet(place(p_at(hub, e), p)))
+        away(q, q_at(turn(pl_), e), lambda: greet(place(q, q_at(turn(pl_), e))))
 
     loop(0, 2, greet_turn)
-    same = jnp.where(jnp.logical_and(p == q, ql == pl_), 1, 0)
+    same = jnp.where(jnp.logical_and(p == q, ql == 0), 1, 0)
 
     slot = [member(mem, k) // 8 for k in range(STEPS)]
     fetches[0].wait()
@@ -308,7 +313,7 @@
 
     def t1_copy(k, e, at):
         return copy(
-            mine.at[k], raw.at[1 - f, f, at, k], snd_t1.at[k, e], rcv_t.at[k, at], place(p_at(ql, e), p)
+            mine.at[k], raw.at[1 - f, f, at, k], snd_t1.at[k, e], rcv_t.at[k, at], place(p_at(hub, e), p)
         )
 
     def t2_copy(k, e, line, at):
@@ -343,10 +348,10 @@
 
         r1_copy(k, q).start()
         for e in range(2):
-            away(p_at(ql, e), p, lambda: t1_copy(k, e, q).start())
+            away(p_at(hub, e), p, lambda: t1_copy(k, e, q).start())
         raw[f, f, q, k] = mine[k]
 
-        @pl.when(jnp.logical_and(p == q, ql == pl_))
+        @pl.when(jnp.logical_and(p == q, ql == 0))
         def _():
             raw[1 - f, f, q, k] = mine[k]
 
@@ -355,13 +360,13 @@
         for e in range(2):
             loop(1, 4, lambda d: r2_copy(k, e, q_line(d), q_at(ql, e)).start())
         for e in range(2):
-            at = q_at(pl_, e)
+            at = q_at(turn(pl_), e)
             away(q, at, lambda: t1_copy(k, e, at).wait_recv())
             loop(1, 4, lambda d: t2_copy(k, e, p_line(d), at).start())
         if k:
             for e in range(2):
                 x_copy(f, q_at(ql, e), f).start()
-                x_copy(1 - f, q_at(pl_, e), f).start()
+                x_copy(1 - f, q_at(turn(pl_), e), f).start()
 
     for h in range(2):
         loop(1, 8, lambda d: s1_copy(h, q_peer(d), q).start())
@@ -505,7 +510,7 @@
             for k in range(2):
                 r2_copy(k, e, q_line(d), at).wait_recv()
             x_copy(f, at, f).start()
-            at = q_at(p_line(d), e)
+            at = q_at(turn(p_line(d)), e)
             for k in range(2):
                 t2_copy(k, e, p_line(d), at).wait_recv()
             x_copy(1 - f, at, f).start()
@@ -572,13 +577,13 @@
     for k in range(2):
         r1_copy(k, q).wait_send()
         for e in range(2):
-            away(p_at(ql, e), p, lambda: t1_copy(k, e, q).wait_send())
+            away(p_at(hub, e), p, lambda: t1_copy(k, e, q).wait_send())
 
     def tail_line(d):
         for k in range(2):
             for e in range(2):
                 r2_copy(k, e, q_line(d), q_at(ql, e)).wait_send()
-                t2_copy(k, e, p_line(d), q_at(pl_, e)).wait_send()
+                t2_copy(k, e, p_line(d), q_at(turn(pl_), e)).wait_send()
 
     loop(1, 4, tail_line)
 

time: 86.8 us -> 79.5 us (0.916)
  Pallas kernels: 84.2 us -> 76.3 us
    pallas_call x1, Pallas kernels: 74.6 us -> 66.7 us  [exchange(): pl.pallas_call(exchange_kernel, out_shape=(jax.ShapeDtypeStruct((1024, 3...]
where the time goes in v7:
time: 79.5 us; the launch traced here: 78.8 us
  Pallas kernels  76.3 us (96%)
  local copies, waits for them, and re-layouts  1.8 us (2%)
    pallas_call x1, Pallas kernels, exchange(): pl.pallas_call(exchange_kernel, out_shape=(jax.ShapeDtypeStruct((1024, 3...  66.7 us
    pallas_call x1, Pallas kernels, update(): pl.pallas_call(update_kernel, out_shape=(jax.ShapeDtypeStruct(hess.shape,...  9.61 us
    unnamed x6, local copies, waits for them, and re-layouts  1.8 us

profile of v7, /device:TPU:105, one launch (start us, length us, event | category | flops | bytes accessed | tf_op | source)
XLA Modules:
  0.0 78.8 jit_solution(5866627359690156168)
XLA Ops:
  0.6 0.0 copy-start
  0.6 0.0 copy-start.1
  0.7 0.9 %copy-done.1 = s32[64,64]{1,0:T(8,128)S(1)} copy-done((s32[64,64]{1,0:T(8,128)S(1)}, s32[64,64]{1,0:T(8,128)}, u32[]{:S(2)}) %copy-start.1) | copy-done | bytes 16408
  1.6 0.0 copy-start.2
  1.6 0.9 %copy-done.2 = s32[2,2]{1,0:T(2,128)S(1)} copy-done((s32[2,2]{1,0:T(2,128)S(1)}, s32[2,2]{1,0:T(2,128)}, u32[]{:S(2)}) %copy-start.2) | copy-done | bytes 40
  2.5 66.7 %exchange.1 = (bf16[1024,1536]{1,0:T(8,128)(2,1)S(1)}, bf16[1024,1536]{1,0:T(8,128)(2,1)S(1)}, f32[4,128,128]{2,1,0:T(8,128)S(1)}, f32[8,512]{1,0:T(8,128)S(1)}, f32[8,8,128]{2,1,0:T(8,128)S(1)}) custom-call(s32[2,2]{1,0:T(2,128)S(1)} %copy-done.2, s32[64,64]{1,0:T(8,128)S(1)} %copy-done.1, f32[8,1024,128]{2,1,0:T(8,128)} %bitcast.10, ...), custom_call_target="tpu_custom_call" | custom-call | tf_op jit(solution)/shard_map/exchange/pallas_call | solution.py:602
  69.2 0.0 copy-done
  69.2 9.6 %update.1 = (f32[8,1024,128]{2,1,0:T(8,128)}, f32[8,128]{1,0:T(8,128)}) custom-call(s32[2,2]{1,0:T(2,128)S(1)} %copy-done.2, s32[64,64]{1,0:T(8,128)S(1)} %copy-done.1, f32[4,128,128]{2,1,0:T(8,128)S(1)} %get-tuple-element.9.diag, bf16[1024,1536]{1,0:T(8,128)(2,1)S(1)} %get-tuple-element.10.x_row, bf16[1024,1536]{1,0:T(8,128)(2,1)S(1)} %get-tuple-element.11.x_col, ...), custom_call_target="tpu_custom_call" | custom-call | tf_op jit(solution)/shard_map/update/pallas_call | solution.py:729
Async XLA Ops:
  0.6 68.5 %copy-start = (f32[8,1,128,8,1,128]{5,4,3,2,1,0:T(1,128)S(1)}, f32[8,1,128,8,1,128]{5,4,3,2,1,0:T(1,128)}, u32[]{:S(2)}) copy-start(f32[8,1,128,8,1,128]{5,4,3,2,1,0:T(1,128)} %param.15) | copy-start | bytes 12582916
  0.6 0.9 %copy-start.1 = (s32[64,64]{1,0:T(8,128)S(1)}, s32[64,64]{1,0:T(8,128)}, u32[]{:S(2)}) copy-start(s32[64,64]{1,0:T(8,128)} %pat.3) | copy-start | bytes 49156
  1.6 0.9 %copy-start.2 = (s32[2,2]{1,0:T(2,128)S(1)}, s32[2,2]{1,0:T(2,128)}, u32[]{:S(2)}) copy-start(s32[2,2]{1,0:T(2,128)} %mem.3) | copy-start | bytes 52

commit v8 on v7

--- a/solution.py
+++ b/solution.py
@@ -655,18 +655,12 @@
     )(mem, pat, *(pltpu.with_memory_space_constraint(x, pltpu.HBM) for x in operands))
 
 
-def update_kernel(mem, pat, diag, x_row, x_col, y, g, hess, out, grad_out, rows, in_sem, out_sem):
+def update_kernel(mem, pat, diag, x_row, x_col, y, g, hess, out, grad_out, rows, out_sem):
     r = lax.axis_index("prow")
     c = lax.axis_index("pcol")
 
-    def load(a):
-        return pltpu.make_async_copy(hess.at[a], rows.at[a], in_sem.at[a])
-
     def save(a):
         return pltpu.make_async_copy(rows.at[a], out.at[a], out_sem.at[a])
-
-    for a in range(8):
-        load(a).start()
 
     def is_pivot(i):
         pivot = i == member(mem, 0)
@@ -674,13 +668,17 @@
             pivot = jnp.logical_or(pivot, i == member(mem, k))
         return pivot
 
-    dec = dot3(split(jnp.concatenate([y[...], y[...]], axis=0)), (x_row[:, 0:WIDE], x_row[:, WIDE : 2 * WIDE]))
-    for a in range(8):
-        i = 8 * a + r
-        val = g[a, pl.ds(r, 1), :] - dec[0:1, BS * a : BS * a + BS]
+    def gradient(a, i):
+        mine = pl.ds(pl.multiple_of(BS * a, BS), BS)
+        part = jnp.zeros((BS, BS), f32)
+        for k in range(STEPS):
+            hi = x_row[mine, BS * k : BS * k + BS].astype(f32)
+            rest = x_row[mine, WIDE + BS * k : WIDE + BS * k + BS].astype(f32)
+            part = part + (hi + rest) * y[0:1, BS * k : BS * k + BS]
+        val = g[a, pl.ds(r, 1), :] - jnp.sum(part.T, axis=0, keepdims=True)
         for k in range(STEPS):
             val = jnp.where(i == member(mem, k), y[0:1, BS * k : BS * k + BS], val)
-        grad_out[a : a + 1, :] = val
+        grad_out[pl.ds(a, 1), :] = val
 
     rr = lax.broadcasted_iota(jnp.int32, (BS, BS), 0)
     cc = lax.broadcasted_iota(jnp.int32, (BS, BS), 1)
@@ -692,15 +690,15 @@
         for e in range(2):
             a = 2 * t + e
             i = 8 * a + r
+            gradient(a, i)
             live = jnp.where(is_pivot(i), 0.0, 1.0).astype(f32)
-            load(a).wait()
             for b in range(8):
                 j = 8 * b + c
                 keep = live * pat[i, j].astype(f32)
                 on = jnp.where(i == j, 1.0, 0.0).astype(f32) * live
                 sub = upd[BS * e : BS * e + BS, BS * b : BS * b + BS]
                 there = pl.ds(b, BS, stride=8)
-                rows[a, there, :] = keep * (rows[a, there, :] - sub) + on * shift
+                rows[a, there, :] = keep * (hess[a, there, :] - sub) + on * shift
             for k in range(STEPS):
                 pk = member(mem, k)
 
@@ -732,11 +730,10 @@
             jax.ShapeDtypeStruct(hess.shape, f32),
             jax.ShapeDtypeStruct((8, BS), f32),
         ),
-        in_specs=[SM, SM, VM, VM, VM, VM, VM, ANY],
+        in_specs=[SM, SM, VM, VM, VM, VM, VM, VM],
         out_specs=(ANY, VM),
         scratch_shapes=[
             pltpu.VMEM((8, 1024, BS), f32),
-            pltpu.SemaphoreType.DMA((8,)),
             pltpu.SemaphoreType.DMA((8,)),
         ],
         compiler_params=pltpu.CompilerParams(vmem_limit_bytes=32 << 20),

time: 79.5 us -> 78.5 us (0.987)
  Pallas kernels: 76.3 us -> 75.3 us
    pallas_call x1, Pallas kernels: 9.61 us -> 8.55 us  [update(): pl.pallas_call(update_kernel, out_shape=(jax.ShapeDtypeStruct(hess.shape,...]
where the time goes in v8:
time: 78.5 us; the launch traced here: 77.7 us
  Pallas kernels  75.3 us (96%)
  local copies, waits for them, and re-layouts  1.8 us (2%)
    pallas_call x1, Pallas kernels, exchange(): pl.pallas_call(exchange_kernel, out_shape=(jax.ShapeDtypeStruct((1024, 3...  66.7 us
    pallas_call x1, Pallas kernels, update(): pl.pallas_call(update_kernel, out_shape=(jax.ShapeDtypeStruct(hess.shape,...  8.55 us
    unnamed x6, local copies, waits for them, and re-layouts  1.8 us

profile of v8, /device:TPU:105, one launch (start us, length us, event | category | flops | bytes accessed | tf_op | source)
XLA Modules:
  0.0 77.7 jit_solution(16673889777841410633)
XLA Ops:
  0.6 0.0 copy-start
  0.6 0.0 copy-start.1
  0.7 0.9 %copy-done.1 = s32[64,64]{1,0:T(8,128)S(1)} copy-done((s32[64,64]{1,0:T(8,128)S(1)}, s32[64,64]{1,0:T(8,128)}, u32[]{:S(2)}) %copy-start.1) | copy-done | bytes 16408
  1.6 0.0 copy-start.2
  1.6 0.9 %copy-done.2 = s32[2,2]{1,0:T(2,128)S(1)} copy-done((s32[2,2]{1,0:T(2,128)S(1)}, s32[2,2]{1,0:T(2,128)}, u32[]{:S(2)}) %copy-start.2) | copy-done | bytes 40
  2.5 66.7 %exchange.1 = (bf16[1024,1536]{1,0:T(8,128)(2,1)S(1)}, bf16[1024,1536]{1,0:T(8,128)(2,1)S(1)}, f32[4,128,128]{2,1,0:T(8,128)S(1)}, f32[8,512]{1,0:T(8,128)S(1)}, f32[8,8,128]{2,1,0:T(8,128)S(1)}) custom-call(s32[2,2]{1,0:T(2,128)S(1)} %copy-done.2, s32[64,64]{1,0:T(8,128)S(1)} %copy-done.1, f32[8,1024,128]{2,1,0:T(8,128)} %bitcast.10, ...), custom_call_target="tpu_custom_call" | custom-call | tf_op jit(solution)/shard_map/exchange/pallas_call | solution.py:602
  69.2 0.0 copy-done
  69.2 8.5 %update.1 = (f32[8,1024,128]{2,1,0:T(8,128)}, f32[8,128]{1,0:T(8,128)}) custom-call(s32[2,2]{1,0:T(2,128)S(1)} %copy-done.2, s32[64,64]{1,0:T(8,128)S(1)} %copy-done.1, f32[4,128,128]{2,1,0:T(8,128)S(1)} %get-tuple-element.9.diag, bf16[1024,1536]{1,0:T(8,128)(2,1)S(1)} %get-tuple-element.10.x_row, bf16[1024,1536]{1,0:T(8,128)(2,1)S(1)} %get-tuple-element.11.x_col, ...), custom_call_target="tpu_custom_call" | custom-call | tf_op jit(solution)/shard_map/update/pallas_call | solution.py:727
Async XLA Ops:
  0.6 68.5 %copy-start = (f32[8,1,128,8,1,128]{5,4,3,2,1,0:T(1,128)S(1)}, f32[8,1,128,8,1,128]{5,4,3,2,1,0:T(1,128)}, u32[]{:S(2)}) copy-start(f32[8,1,128,8,1,128]{5,4,3,2,1,0:T(1,128)} %param.15) | copy-start | bytes 12582916
  0.6 0.9 %copy-start.1 = (s32[64,64]{1,0:T(8,128)S(1)}, s32[64,64]{1,0:T(8,128)}, u32[]{:S(2)}) copy-start(s32[64,64]{1,0:T(8,128)} %pat.3) | copy-start | bytes 49156
  1.6 0.9 %copy-start.2 = (s32[2,2]{1,0:T(2,128)S(1)}, s32[2,2]{1,0:T(2,128)}, u32[]{:S(2)}) copy-start(s32[2,2]{1,0:T(2,128)} %mem.3) | copy-start | bytes 52

commit v9 on v8

--- a/solution.py
+++ b/solution.py
@@ -133,13 +133,13 @@
 
 
 def exchange_kernel(
-    mem, pat, hess_at, poses_at, codebook_at, offsets_at, conf_at, codes_at, kinds_at,
+    mem_at, pat_at, hess_at, poses_at, codebook_at, offsets_at, conf_at, codes_at, kinds_at,
     x_row, x_col, diag, y_out, g_out,
     hess, poses, codebook, offsets, conf, codes, kinds, scand, ccand, pg, s_all, low, inv, fac_u, fac_i, raw, wh, wl,
     s1r_a, s1r_b, s1, s2r_a, s2r_b, par_a, par_b, picked, both_a, both_b, mine, g1r, g1, g2r, g2, g3r,
     snd_s1, rcv_s1, snd_s2, rcv_s2, snd_s3, rcv_s3, snd_sx, rcv_sx,
     snd_x, rcv_x, snd_a, rcv_a, snd_r2, snd_t2, snd_t1, rcv_r, rcv_t,
-    snd_g1, rcv_g1, snd_g2, rcv_g2, snd_g4, rcv_g4, snd_g3, rcv_g3, snd_b, rcv_b, snd_r1, in_sem,
+    snd_g1, rcv_g1, snd_g2, rcv_g2, snd_g4, rcv_g4, snd_g3, rcv_g3, snd_b, rcv_b, snd_r1, in_sem, mem, pat,
 ):
     fetches = [
         pltpu.make_async_copy(src, dst, in_sem.at[n])
@@ -147,10 +147,11 @@
             [
                 (hess_at, hess), (codes_at, codes), (conf_at, conf), (kinds_at, kinds),
                 (poses_at, poses), (codebook_at, codebook), (offsets_at, offsets),
+                (mem_at, mem), (pat_at, pat),
             ]
         )
     ]
-    for fetch in fetches:
+    for fetch in fetches[7:] + fetches[:7]:
         fetch.start()
     s1r, s2r = (s1r_a, s1r_b), (s2r_a, s2r_b)
     par, both = (par_a, par_b), (both_a, both_b)
@@ -236,8 +237,9 @@
     loop(0, 2, greet_turn)
     same = jnp.where(jnp.logical_and(p == q, ql == 0), 1, 0)
 
+    fetches[7].wait()
+    fetches[0].wait()
     slot = [member(mem, k) // 8 for k in range(STEPS)]
-    fetches[0].wait()
     for e, (k, m) in enumerate(PAIRS):
         scand[e] = hess[slot[k], pl.ds(slot[m], BS, stride=8), :]
 
@@ -378,7 +380,7 @@
     for e in range(2):
         for k in range(2):
             par[k][ql, e] = ccand[q_at(ql, e), k]
-    for fetch in fetches[1:]:
+    for fetch in fetches[1:7] + fetches[8:]:
         fetch.wait()
     moment = moments(poses, codebook, offsets, conf, codes, kinds)
     for half in range(2):
@@ -608,7 +610,7 @@
             jax.ShapeDtypeStruct((8, WIDE), f32),
             jax.ShapeDtypeStruct((8, 8, BS), f32),
         ),
-        in_specs=[SM, SM] + [HBM] * 7,
+        in_specs=[HBM] * 9,
         out_specs=(VM,) * 5,
         scratch_shapes=[vmem(x.shape, x.dtype) for x in operands]
         + [
@@ -647,12 +649,12 @@
         + [sem((8,))] * 6
         + [sem] * 2
         + [sem((2,))] * 3
-        + [sem((7,))],
+        + [sem((9,)), pltpu.SMEM(mem.shape, jnp.int32), pltpu.SMEM(pat.shape, jnp.int32)],
         compiler_params=pltpu.CompilerParams(
             collective_id=0, has_side_effects=True, vmem_limit_bytes=40 << 20
         ),
         name="exchange",
-    )(mem, pat, *(pltpu.with_memory_space_constraint(x, pltpu.HBM) for x in operands))
+    )(*(pltpu.with_memory_space_constraint(x, pltpu.HBM) for x in (mem, pat, *operands)))
 
 
 def update_kernel(mem, pat, diag, x_row, x_col, y, g, hess, out, grad_out, rows, out_sem):

time: 78.5 us -> 75.7 us (0.964)
  local copies, waits for them, and re-layouts: 1.8 us -> 0.01 us
  Pallas kernels: 75.3 us -> 74.3 us
    unnamed x6, local copies, waits for them, and re-layouts: 1.8 us -> 0.01 us
    pallas_call x1, Pallas kernels: 66.7 us -> 65.9 us  [exchange(): pl.pallas_call(exchange_kernel, out_shape=(jax.ShapeDtypeStruct((1024, 3...]
where the time goes in v9:
time: 75.7 us; the launch traced here: 75 us
  Pallas kernels  74.3 us (98%)
    pallas_call x1, Pallas kernels, exchange(): pl.pallas_call(exchange_kernel, out_shape=(jax.ShapeDtypeStruct((1024, 3...  65.9 us
    pallas_call x1, Pallas kernels, update(): pl.pallas_call(update_kernel, out_shape=(jax.ShapeDtypeStruct(hess.shape,...  8.42 us

profile of v9, /device:TPU:105, one launch (start us, length us, event | category | flops | bytes accessed | tf_op | source)
XLA Modules:
  0.0 75.0 jit_solution(13214955245720041304)
XLA Ops:
  0.6 0.0 copy-start.2
  0.6 0.0 copy-start.1
  0.7 0.0 copy-start
  0.7 65.9 %exchange.1 = (bf16[1024,1536]{1,0:T(8,128)(2,1)S(1)}, bf16[1024,1536]{1,0:T(8,128)(2,1)S(1)}, f32[4,128,128]{2,1,0:T(8,128)S(1)}, f32[8,512]{1,0:T(8,128)S(1)}, f32[8,8,128]{2,1,0:T(8,128)S(1)}) custom-call(s32[2,2]{1,0:T(2,128)} %mem.1, s32[64,64]{1,0:T(8,128)} %pat.1, f32[8,1024,128]{2,1,0:T(8,128)} %bitcast.10, bf16[2048,256]{1,0:T(8,128)(2,1)} %poses_at.1, ...), custom_call_target="tpu_custom_call" | custom-call | tf_op jit(solution)/shard_map/exchange/pallas_call | solution.py:604
  66.5 0.0 copy-done.2
  66.6 0.0 copy-done.1
  66.6 0.0 copy-done
  66.6 8.4 %update.1 = (f32[8,1024,128]{2,1,0:T(8,128)}, f32[8,128]{1,0:T(8,128)}) custom-call(s32[2,2]{1,0:T(2,128)S(1)} %copy-done.2, s32[64,64]{1,0:T(8,128)S(1)} %copy-done.1, f32[4,128,128]{2,1,0:T(8,128)S(1)} %get-tuple-element.9.diag, bf16[1024,1536]{1,0:T(8,128)(2,1)S(1)} %get-tuple-element.10.x_row, bf16[1024,1536]{1,0:T(8,128)(2,1)S(1)} %get-tuple-element.11.x_col, ...), custom_call_target="tpu_custom_call" | custom-call | tf_op jit(solution)/shard_map/update/pallas_call | solution.py:729
Async XLA Ops:
  0.6 65.9 %copy-start.2 = (s32[2,2]{1,0:T(2,128)S(1)}, s32[2,2]{1,0:T(2,128)}, u32[]{:S(2)}) copy-start(s32[2,2]{1,0:T(2,128)} %mem.1) | copy-start | bytes 52
  0.6 65.9 %copy-start.1 = (s32[64,64]{1,0:T(8,128)S(1)}, s32[64,64]{1,0:T(8,128)}, u32[]{:S(2)}) copy-start(s32[64,64]{1,0:T(8,128)} %pat.1) | copy-start | bytes 49156
  0.7 65.9 %copy-start = (f32[8,1,128,8,1,128]{5,4,3,2,1,0:T(1,128)S(1)}, f32[8,1,128,8,1,128]{5,4,3,2,1,0:T(1,128)}, u32[]{:S(2)}) copy-start(f32[8,1,128,8,1,128]{5,4,3,2,1,0:T(1,128)} %param.15) | copy-start | bytes 12582916

commit v10 on v9

--- a/solution.py
+++ b/solution.py
@@ -348,9 +348,9 @@
         def _():
             mine[k] = both[k][lax.rem(mem[1, k], 8) // 4].T
 
+        for e in range(2):
+            away(p_at(hub, e), p, lambda: t1_copy(k, e, q).start())
         r1_copy(k, q).start()
-        for e in range(2):
-            away(p_at(hub, e), p, lambda: t1_copy(k, e, q).start())
         raw[f, f, q, k] = mine[k]
 
         @pl.when(jnp.logical_and(p == q, ql == 0))

time: 75.7 us -> 75.8 us (level)
  no operation moved by 1% of the time
where the time goes in v10:
time: 75.8 us; the launch traced here: 75.1 us
  Pallas kernels  74.4 us (98%)
    pallas_call x1, Pallas kernels, exchange(): pl.pallas_call(exchange_kernel, out_shape=(jax.ShapeDtypeStruct((1024, 3...  65.9 us
    pallas_call x1, Pallas kernels, update(): pl.pallas_call(update_kernel, out_shape=(jax.ShapeDtypeStruct(hess.shape,...  8.58 us

profile of v10, /device:TPU:105, one launch (start us, length us, event | category | flops | bytes accessed | tf_op | source)
XLA Modules:
  0.0 75.1 jit_solution(11208285733854929790)
XLA Ops:
  0.6 0.0 copy-start.2
  0.6 0.0 copy-start.1
  0.7 0.0 copy-start
  0.7 65.9 %exchange.1 = (bf16[1024,1536]{1,0:T(8,128)(2,1)S(1)}, bf16[1024,1536]{1,0:T(8,128)(2,1)S(1)}, f32[4,128,128]{2,1,0:T(8,128)S(1)}, f32[8,512]{1,0:T(8,128)S(1)}, f32[8,8,128]{2,1,0:T(8,128)S(1)}) custom-call(s32[2,2]{1,0:T(2,128)} %mem.1, s32[64,64]{1,0:T(8,128)} %pat.1, f32[8,1024,128]{2,1,0:T(8,128)} %bitcast.10, bf16[2048,256]{1,0:T(8,128)(2,1)} %poses_at.1, ...), custom_call_target="tpu_custom_call" | custom-call | tf_op jit(solution)/shard_map/exchange/pallas_call | solution.py:604
  66.5 0.0 copy-done.2
  66.5 0.0 copy-done.1
  66.5 0.0 copy-done
  66.6 8.6 %update.1 = (f32[8,1024,128]{2,1,0:T(8,128)}, f32[8,128]{1,0:T(8,128)}) custom-call(s32[2,2]{1,0:T(2,128)S(1)} %copy-done.2, s32[64,64]{1,0:T(8,128)S(1)} %copy-done.1, f32[4,128,128]{2,1,0:T(8,128)S(1)} %get-tuple-element.9.diag, bf16[1024,1536]{1,0:T(8,128)(2,1)S(1)} %get-tuple-element.10.x_row, bf16[1024,1536]{1,0:T(8,128)(2,1)S(1)} %get-tuple-element.11.x_col, ...), custom_call_target="tpu_custom_call" | custom-call | tf_op jit(solution)/shard_map/update/pallas_call | solution.py:729
Async XLA Ops:
  0.6 65.9 %copy-start.2 = (s32[2,2]{1,0:T(2,128)S(1)}, s32[2,2]{1,0:T(2,128)}, u32[]{:S(2)}) copy-start(s32[2,2]{1,0:T(2,128)} %mem.1) | copy-start | bytes 52
  0.6 65.9 %copy-start.1 = (s32[64,64]{1,0:T(8,128)S(1)}, s32[64,64]{1,0:T(8,128)}, u32[]{:S(2)}) copy-start(s32[64,64]{1,0:T(8,128)} %pat.1) | copy-start | bytes 49156
  0.7 65.9 %copy-start = (f32[8,1,128,8,1,128]{5,4,3,2,1,0:T(1,128)S(1)}, f32[8,1,128,8,1,128]{5,4,3,2,1,0:T(1,128)}, u32[]{:S(2)}) copy-start(f32[8,1,128,8,1,128]{5,4,3,2,1,0:T(1,128)} %param.15) | copy-start | bytes 12582916
